TPU v7x, 768 devices: a whole 4x8x12 slice. The times are simulated.
768 devices in a mesh: region: 768 (over x, z, y, core).
Axes of the slice: x: 4, y: 8, z: 12, core: 2. Of those that a mesh axis runs over, the one named last changes fastest.
Arguments:
- coefficients: float32 [9, 35, 98304], P(None, None, 'region'), may hold values from -6 to 6
- star_matrices: float32 [3, 9, 9, 98304], P(None, None, None, 'region'), may hold values from -4.4 to 4.4
- flux_solvers: float32 [2, 4, 9, 9, 98304], P(None, None, None, None, 'region'), may hold values from -2 to 2
- stiffness: float32 [3, 35, 35], replicated, may hold values from -1 to 1
- projection: float32 [4, 15, 35], replicated, may hold values from -1 to 1
- lifting: float32 [4, 35, 15], replicated, may hold values from -1 to 1
- block_cluster: int32 [6144], P('region'), may hold values from 0 to 2, as said below
- neighbors: int32 [4, 98304], P(None, 'region'), may hold values from 0 to 767, as said below
- send_faces: int32 [4, 49152], P(None, 'region'), may hold values from 0 to 511, as said below
Outputs:
- updated: float32 [9, 35, 98304], P(None, None, 'region')
Inputs may be any that keep to these rules, and one draw needn't show every extreme that they name: `block_cluster`: the cluster of each block of 16 consecutive elements of a device, blocks in the device's order. `neighbors`: entry [f, e] of a device is a column of that device's face table: f2 * 128 + e2 for a face f2 of an element e2 of the same device (the face itself for faces on the outer surface and for faces listed toward a device beyond the ends of the curve), or 512 + k * 64 + j for the face in slot j of the device's list k, when the device r + o(k), o = (-1, -2, 2, 1), exists. Faces paired within a device name each other. `send_faces`: list k of a device holds 64 distinct faces f * 128 + e of that device, no face in two lists; slot j of list k of device r meets slot j of list 3 - k of device r + o(k), o = (-1, -2, 2, 1).
All inputs are finite; a program needn't handle non-finite values.
Results may differ from a plain program's by a relative error of at most 0.0003.
Values sent between devices are 32-bit elements; how exact they have to be, the bound alone decides.
No kernel may reach another device: no remote copies, remote signals or barrier semaphores. Data moves between devices by JAX's collectives and lax.ppermute only.
A program may use at most 64 MiB of HBM per device.

v0:
```python
import functools

import jax
import jax.numpy as jnp
from jax import lax
from jax.experimental import pallas as pl
from jax.experimental.pallas import tpu as pltpu
from jax.sharding import PartitionSpec as P

NQ = 9
BASIS = 35
ROWS = 40
FACES = 4
FACE_BASIS = 15
FACE_ROWS = 16
DERIVS = 5
TICKS = 4
LANES = 128
BLOCK = 16
STEP = 0.125
FACTORIALS = (1.0, 2.0, 6.0, 24.0, 120.0)
F32 = jnp.float32
BF16 = jnp.bfloat16
TABLE = NQ * FACE_ROWS
WIDE = NQ * LANES


def split_pair(x):
    high = x.astype(BF16)
    return high, (x - high.astype(F32)).astype(BF16)


def stacked(x, depth):
    high = x.astype(BF16).astype(F32)
    parts = [high, x - high, high]
    rest = depth - 3 * x.shape[0]
    if rest:
        parts.append(jnp.zeros((rest, x.shape[1]), F32))
    return jnp.concatenate(parts, axis=0).astype(BF16)


def placed(block, offset, width, rows):
    source = lax.broadcasted_iota(jnp.int32, (block.shape[1], width), 0)
    target = lax.broadcasted_iota(jnp.int32, (block.shape[1], width), 1)
    chosen = (target == source + offset).astype(BF16)
    return jnp.dot(block, chosen, preferred_element_type=F32)


def weights_into(ref, row, block, stride):
    high, low = split_pair(block)
    width = ref.shape[1]
    full = (
        placed(high, 0, width, 0) + placed(high, stride, width, 0) + placed(low, 2 * stride, width, 0)
    )
    ref[row : row + block.shape[0], :] = full


def wide(ref):
    return jnp.concatenate([ref[q] for q in range(NQ)], axis=1)


def matmul(weights, x):
    return jnp.dot(weights, x, preferred_element_type=F32)


def contract_star(blocks, base, star_ref, finish):
    for first in range(0, NQ, 3):
        totals = [None] * 3
        for direction in range(3):
            for source in range(NQ):
                block = blocks[
                    base + direction * ROWS : base + (direction + 1) * ROWS,
                    source * LANES : (source + 1) * LANES,
                ]
                for k in range(3):
                    term = block * star_ref[direction, source, first + k : first + k + 1, :]
                    totals[k] = term if totals[k] is None else totals[k] + term
        for k in range(3):
            finish(first + k, totals[k])


def tick_weights(period, tick):
    out = []
    for k in range(DERIVS):
        values = []
        for p in (1, 2, 4):
            s = STEP * (tick % p)
            values.append(((s + STEP) ** (k + 1) - s ** (k + 1)) / FACTORIALS[k])
        out.append(jnp.where(period == 1, values[0], jnp.where(period == 2, values[1], values[2])))
    return out


def own_weights(period):
    out = []
    for k in range(DERIVS):
        values = [(STEP * p) ** (k + 1) / FACTORIALS[k] for p in (1, 2, 4)]
        out.append(jnp.where(period == 1, values[0], jnp.where(period == 2, values[1], values[2])))
    return out


def predict_and_send(
    tick, first_state, star_ref, stiff_ref, proj_ref, send_ref, period_ref,
    table_ref, own_ref, near_list_ref, far_list_ref, derivs, blocks, faces,
):
    def degree(k, carry):
        x = jnp.concatenate([derivs[k, q] for q in range(NQ)], axis=1)
        blocks[...] = matmul(stiff_ref[...], stacked(x, LANES))

        def finish(p, total):
            derivs[k + 1, p] = total

        contract_star(blocks, 0, star_ref, finish)
        return carry

    lax.fori_loop(0, DERIVS - 1, degree, 0)
    period = period_ref[0:1, :]
    now = tick_weights(period, tick)
    whole = own_weights(period)
    parts = []
    for q in range(NQ):
        tick_sum = None
        own_sum = None
        for k in range(DERIVS):
            d = derivs[k, q]
            a, b = d * now[k], d * whole[k]
            tick_sum = a if tick_sum is None else tick_sum + a
            own_sum = b if own_sum is None else own_sum + b
        own_ref[q] = own_sum
        parts.append(tick_sum)
    faces[...] = matmul(proj_ref[...], stacked(jnp.concatenate(parts, axis=1), LANES))
    highs, lows = [], []
    for q in range(NQ):
        row = jnp.concatenate(
            [
                faces[f * FACE_ROWS : (f + 1) * FACE_ROWS, q * LANES : (q + 1) * LANES]
                for f in range(FACES)
            ],
            axis=1,
        )
        high, low = split_pair(row)
        table_ref[q * FACE_ROWS : (q + 1) * FACE_ROWS, :] = high
        table_ref[TABLE + q * FACE_ROWS : TABLE + (q + 1) * FACE_ROWS, :] = low
    both = matmul(table_ref[...], send_ref[...])
    picked = both[:TABLE] + both[TABLE:]
    near_list_ref[...] = picked[:, :LANES]
    far_list_ref[...] = picked[:, LANES:]


def begin_kernel(
    coef_ref, star_ref, stiffness_ref, projection_ref, cluster_ref, faces_ref,
    state_ref, own_ref, table_ref, near_list_ref, far_list_ref,
    stiff_ref, proj_ref, send_ref, period_ref,
    derivs, blocks, faces, work,
):
    lane = lax.broadcasted_iota(jnp.int32, (8, LANES), 1)
    period = jnp.full((8, LANES), 1, jnp.int32)
    for j in range(LANES // BLOCK):
        c = cluster_ref[j]
        p = jnp.where(c == 0, 1, jnp.where(c == 1, 2, 4))
        period = jnp.where(lane // BLOCK == j, p, period)
    period_ref[...] = period
    derivs[0] = jnp.zeros((NQ, ROWS, LANES), F32)
    for q in range(NQ):
        derivs[0, q, 0:BASIS, :] = coef_ref[q]
    state_ref[...] = derivs[0]
    work[...] = jnp.zeros_like(work)
    for d in range(3):
        weights_into(work, d * ROWS, -stiffness_ref[d], ROWS)
    stiff_ref[...] = work[0 : 3 * ROWS, :].astype(BF16)
    work[...] = jnp.zeros_like(work)
    for f in range(FACES):
        weights_into(work, f * FACE_ROWS, projection_ref[f], ROWS)
    proj_ref[...] = work[0 : FACES * FACE_ROWS, :].astype(BF16)
    column = lax.broadcasted_iota(jnp.int32, (FACES * LANES, LANES), 0)
    near = jnp.concatenate([faces_ref[3:4, :], faces_ref[0:1, :]], axis=1)
    far = jnp.concatenate([faces_ref[1:2, :], faces_ref[2:3, :]], axis=1)
    send_ref[:, :LANES] = (column == near).astype(F32).astype(BF16)
    send_ref[:, LANES:] = (column == far).astype(F32).astype(BF16)
    predict_and_send(
        0, None, star_ref, stiff_ref, proj_ref, send_ref, period_ref,
        table_ref, own_ref, near_list_ref, far_list_ref, derivs, blocks, faces,
    )


def relay_kernel(gathered_ref, far_list_ref, first_ref, second_ref):
    me = lax.axis_index("region")
    other = 1 - lax.rem(me, 2)
    even = lax.rem(me // 2, 2) == 0
    lane = lax.broadcasted_iota(jnp.int32, (TABLE, LANES), 1)
    partner = gathered_ref[other]
    own = far_list_ref[...]
    upward = jnp.where(lane < LANES // 2, partner, own)
    downward = jnp.where(lane < LANES // 2, own, partner)
    first_ref[...] = jnp.where(even, downward, upward)
    second_ref[...] = jnp.where(even, upward, downward)


def face_contract(source, solver_ref, side, into):
    for f in range(FACES):
        totals = [None] * NQ
        for q in range(NQ):
            block = source(q, f)
            for p in range(NQ):
                term = block * solver_ref[side, f, q, p : p + 1, :]
                totals[p] = term if totals[p] is None else totals[p] + term
        for p in range(NQ):
            into[f * FACE_ROWS : (f + 1) * FACE_ROWS, p * LANES : (p + 1) * LANES] = totals[p]


def ending_mask(period, tick):
    return lax.rem(jnp.full_like(period, tick + 1), period) == 0


def own_body(
    tick, state_ref, own_ref, table_ref, sum_ref, star_ref, solver_ref, period_ref,
    both_ref, lift_ref, local_ref, base_ref, partial_ref, big, flux,
):
    ending = ending_mask(period_ref[0:1, :], tick)
    big[...] = matmul(both_ref[...], stacked(wide(own_ref), LANES))
    face_contract(
        lambda q, f: big[f * FACE_ROWS : (f + 1) * FACE_ROWS, q * LANES : (q + 1) * LANES],
        solver_ref, 0, flux,
    )
    lifted = matmul(lift_ref[...], stacked(flux[...], 192))
    def finish(p, total):
        change = total - lifted[:, p * LANES : (p + 1) * LANES]
        base_ref[p] = state_ref[p] + jnp.where(ending, change, 0.0)

    contract_star(big, FACES * FACE_ROWS, star_ref, finish)
    both = matmul(table_ref[...], local_ref[...])
    picked = both[:TABLE] + both[TABLE:]
    partial_ref[...] = picked if sum_ref is None else sum_ref[...] + picked


def own_first_kernel(
    state_ref, own_ref, table_ref, star_ref, solver_ref, period_ref,
    stiffness_ref, projection_ref, lifting_ref, neighbor_ref, order_ref,
    base_ref, partial_ref, both_ref, lift_ref, local_ref, remote_ref,
    big, flux, work, work_lift,
):
    work[...] = jnp.zeros_like(work)
    for f in range(FACES):
        weights_into(work, f * FACE_ROWS, projection_ref[f], ROWS)
    for d in range(3):
        weights_into(work, FACES * FACE_ROWS + d * ROWS, stiffness_ref[d].T, ROWS)
    both_ref[...] = work[...].astype(BF16)
    work_lift[...] = jnp.zeros_like(work_lift)
    lifts = jnp.zeros((BASIS, 192), F32)
    for f in range(FACES):
        high, low = split_pair(lifting_ref[f])
        for part, offset in ((high, 0), (high, 64), (low, 128)):
            lifts = lifts + placed(part, offset + f * FACE_ROWS, 192, 0)
    work_lift[0:BASIS, :] = lifts
    lift_ref[...] = work_lift[...].astype(BF16)
    column = lax.broadcasted_iota(jnp.int32, (LANES, LANES), 0)
    for f in range(FACES):
        row = neighbor_ref[f : f + 1, :]
        for g in range(6):
            chosen = (column + g * LANES == row).astype(F32).astype(BF16)
            if g < FACES:
                local_ref[g * LANES : (g + 1) * LANES, f * LANES : (f + 1) * LANES] = chosen
            else:
                start = (g - FACES) * LANES
                remote_ref[start : start + LANES, f * LANES : (f + 1) * LANES] = chosen
    own_body(
        0, state_ref, own_ref, table_ref, None, star_ref, solver_ref, period_ref,
        both_ref, lift_ref, local_ref, base_ref, partial_ref, big, flux,
    )


def own_kernel(
    tick, state_ref, own_ref, table_ref, sum_ref, star_ref, solver_ref, period_ref,
    both_ref, lift_ref, local_ref, order_ref,
    base_ref, partial_ref, big, flux,
):
    own_body(
        tick, state_ref, own_ref, table_ref, sum_ref, star_ref, solver_ref, period_ref,
        both_ref, lift_ref, local_ref, base_ref, partial_ref, big, flux,
    )


def near_body(
    tick, first_ref, second_ref, gathered_ref, base_ref, partial_ref, solver_ref, period_ref,
    lift_ref, remote_ref, sums, flux,
):
    me = lax.axis_index("region")
    core = lax.rem(me, 2)
    even = lax.rem(me // 2, 2) == 0
    lane = lax.broadcasted_iota(jnp.int32, (TABLE, LANES), 1)
    low_half = lane < LANES // 2
    partner = gathered_ref[1 - core]
    first, second = first_ref[...], second_ref[...]
    upward = jnp.where(even, first, second)
    downward = jnp.where(even, second, first)
    lower = jnp.where(jnp.logical_and(core == 1, low_half), partner, upward)
    upper = jnp.where(
        jnp.logical_and(core == 0, jnp.logical_not(low_half)), partner, downward
    )
    high, low = split_pair(jnp.concatenate([lower, upper], axis=1))
    both = matmul(jnp.concatenate([high, low], axis=0), remote_ref[...])
    sums[...] = partial_ref[...] + both[:TABLE] + both[TABLE:]
    face_contract(
        lambda q, f: sums[q * FACE_ROWS : (q + 1) * FACE_ROWS, f * LANES : (f + 1) * LANES],
        solver_ref, 1, flux,
    )
    return matmul(lift_ref[...], stacked(flux[...], 192))


def step_kernel(
    tick, first_ref, second_ref, gathered_ref, base_ref, partial_ref, star_ref, solver_ref,
    period_ref, lift_ref, remote_ref, stiff_ref, proj_ref, send_ref,
    state_ref, sum_ref, own_ref, table_ref, near_list_ref, far_list_ref,
    sums, flux, derivs, blocks, faces,
):
    lifted = near_body(
        tick, first_ref, second_ref, gathered_ref, base_ref, partial_ref, solver_ref, period_ref,
        lift_ref, remote_ref, sums, flux,
    )
    ending = ending_mask(period_ref[0:1, :], tick)
    for p in range(NQ):
        change = jnp.where(ending, lifted[:, p * LANES : (p + 1) * LANES], 0.0)
        value = base_ref[p] - change
        derivs[0, p] = value
        state_ref[p] = value
    for f in range(FACES):
        part = sums[:, f * LANES : (f + 1) * LANES]
        sum_ref[:, f * LANES : (f + 1) * LANES] = jnp.where(ending, 0.0, part)
    predict_and_send(
        tick + 1, None, star_ref, stiff_ref, proj_ref, send_ref, period_ref,
        table_ref, own_ref, near_list_ref, far_list_ref, derivs, blocks, faces,
    )


def end_kernel(
    first_ref, second_ref, gathered_ref, base_ref, partial_ref, solver_ref,
    period_ref, lift_ref, remote_ref,
    out_ref, sums, flux,
):
    tick = TICKS - 1
    lifted = near_body(
        tick, first_ref, second_ref, gathered_ref, base_ref, partial_ref, solver_ref, period_ref,
        lift_ref, remote_ref, sums, flux,
    )
    ending = ending_mask(period_ref[0:1, :], tick)
    for p in range(NQ):
        change = jnp.where(ending, lifted[:, p * LANES : (p + 1) * LANES], 0.0)
        out_ref[p] = (base_ref[p] - change)[0:BASIS, :]


VMEM = pl.BlockSpec(memory_space=pltpu.VMEM)
SMEM = pl.BlockSpec(memory_space=pltpu.SMEM)


def call(kernel, name, inputs, outputs, scratch, flops, in_specs=None):
    return pl.pallas_call(
        kernel,
        name=name,
        out_shape=[jax.ShapeDtypeStruct(s, d) for s, d in outputs],
        in_specs=in_specs or [VMEM] * len(inputs),
        out_specs=[VMEM] * len(outputs),
        scratch_shapes=[pltpu.VMEM(s, d) for s, d in scratch],
        cost_estimate=pl.CostEstimate(flops=flops, bytes_accessed=flops // 100, transcendentals=0),
        compiler_params=pltpu.CompilerParams(vmem_limit_bytes=24 << 20),
    )(*inputs)


STATE = ((NQ, ROWS, LANES), F32)
PAIRED = ((2 * TABLE, FACES * LANES), BF16)
SUMS = ((TABLE, FACES * LANES), F32)
LIST = ((TABLE, LANES), F32)
DERIV = ((DERIVS, NQ, ROWS, LANES), F32)
BLOCKS = ((3 * ROWS, WIDE), F32)
FACE = ((FACES * FACE_ROWS, WIDE), F32)
BOTH_ROWS = FACES * FACE_ROWS + 3 * ROWS
BIG = ((BOTH_ROWS, WIDE), F32)


def per_device(
    coefficients, star, solvers, stiffness, projection, lifting, block_cluster, neighbors, send_faces
):
    count = lax.axis_size("region")
    cores = [[2 * k, 2 * k + 1] for k in range(count // 2)]
    pairs = ([], [])
    for i in range(count - 2):
        pairs[(i // 2) % 2] .extend([(i, i + 2), (i + 2, i)])
    inner, outer = pairs

    (state, own, table, near_list, far_list, stiff_w, proj_w, send_w, period) = call(
        begin_kernel, "begin",
        (coefficients, star, stiffness, projection, block_cluster, send_faces),
        (
            STATE, STATE, PAIRED, LIST, LIST,
            ((3 * ROWS, LANES), BF16), ((FACES * FACE_ROWS, LANES), BF16),
            ((FACES * LANES, 2 * LANES), BF16), ((8, LANES), jnp.int32),
        ),
        (DERIV, BLOCKS, FACE, ((3 * ROWS, LANES), F32)),
        10**9,
        [VMEM, VMEM, VMEM, VMEM, SMEM, VMEM],
    )
    sums = None
    for tick in range(TICKS):
        gathered = lax.all_gather(near_list, "region", axis_index_groups=cores)
        first, second = call(
            relay_kernel, "relay", (gathered, far_list), (LIST, LIST), (), 10**6
        )
        first_in = lax.ppermute(first, "region", outer)
        second_in = lax.ppermute(second, "region", inner)
        if tick == 0:
            base, partial, both_w, lift_w, local_w, remote_w = call(
                own_first_kernel, "own_first",
                (
                    state, own, table, star, solvers, period,
                    stiffness, projection, lifting, neighbors, first[:8],
                ),
                (
                    STATE, SUMS, ((BOTH_ROWS, LANES), BF16), ((ROWS, 192), BF16),
                    ((FACES * LANES, FACES * LANES), BF16), ((2 * LANES, FACES * LANES), BF16),
                ),
                (BIG, FACE, ((BOTH_ROWS, LANES), F32), ((ROWS, 192), F32)),
                10**9,
            )
        else:
            base, partial = call(
                functools.partial(own_kernel, tick), "own",
                (state, own, table, sums, star, solvers, period, both_w, lift_w, local_w, first[:8]),
                (STATE, SUMS), (BIG, FACE), 10**9,
            )
        if tick < TICKS - 1:
            state, sums, own, table, near_list, far_list = call(
                functools.partial(step_kernel, tick), "step",
                (
                    first_in, second_in, gathered, base, partial, star, solvers,
                    period, lift_w, remote_w, stiff_w, proj_w, send_w,
                ),
                (STATE, SUMS, STATE, PAIRED, LIST, LIST),
                (SUMS, FACE, DERIV, BLOCKS, FACE), 10**9,
            )
    (updated,) = call(
        end_kernel, "end",
        (first_in, second_in, gathered, base, partial, solvers, period, lift_w, remote_w),
        (((NQ, BASIS, LANES), F32),), (SUMS, FACE), 10**9,
    )
    return updated


def solution(mesh):
    placed_specs = (
        P(None, None, "region"),
        P(None, None, None, "region"),
        P(None, None, None, None, "region"),
        P(),
        P(),
        P(),
        P("region"),
        P(None, "region"),
        P(None, "region"),
    )
    return jax.shard_map(
        per_device, mesh=mesh, in_specs=placed_specs, out_specs=P(None, None, "region"),
        check_vma=False,
    )
```

profile of v0, /device:TPU:6, one launch (start us, length us, event | category | flops | bytes accessed | tf_op | source)
XLA Modules:
  0.0 85.4 jit_solution(934211682835702870)
XLA Ops:
  0.0 0.8 copy.11.projection_ref
  0.8 0.0 copy-start.4
  0.8 1.0 %copy.10.star_ref = f32[3,9,9,128]{3,2,1,0:T(8,128)S(1)} copy(f32[3,9,9,128]{3,0,2,1:T(4,128)} %param.10) | data formatting | bytes 248832 | tf_op args[1]
  1.8 3.7 %begin.1 = (f32[9,40,128]{2,1,0:T(8,128)S(1)}, f32[9,40,128]{2,1,0:T(8,128)S(1)}, bf16[288,512]{1,0:T(8,128)(2,1)S(1)}, f32[144,128]{1,0:T(8,128)S(1)}, f32[144,...) custom-call(f32[9,35,128]{2,1,0:T(8,128)S(1)} %copy-done, ...), custom_call_target="tpu_custom_call" | custom-call | flops 1000000000 | bytes 10000000 | tf_op jit(solution)/shard_map/begin/pallas_call | solution.py:355
  5.5 0.0 copy-start.5
  5.5 2.0 %all-gather = f32[288,128]{1,0:T(8,128)S(1)} all-gather(f32[144,128]{1,0:T(8,128)S(1)} %get-tuple-element.52), channel_id=2, replica_groups={{0,1},{2,3},{4,5},{6,7},{8,9},{10,11},{12,13},{14,15},{16,17},{18,19},{..., dimensions={0}, use_global_device_ids=true | all-gather | bytes 221184 | tf_op jit(solution)/shard_map/all_gather | solution.py:402
  7.6 3.5 %collective-permute-start.1 = (f32[144,128]{1,0:T(8,128)S(1)}, f32[144,128]{1,0:T(8,128)S(1)}, u32[]{:S(2)}, u32[]{:S(2)}) collective-permute-start(f32[144,128]{1,0:T(8,128)S(1)} %get-tuple-element.55), channel_id=1, source_target_pairs={{0,2},{2,0},{1,3},{3,1},{4,6},{6,4},{5,7},{7,5},{8,10},{10,8},{9,1... | collective-permute-start | bytes 221192 | tf_op jit(solution)/shard_map/ppermute | solution.py:407
  11.1 17.5 %collective-permute-start = (f32[144,128]{1,0:T(8,128)S(1)}, f32[144,128]{1,0:T(8,128)S(1)}, u32[]{:S(2)}, u32[]{:S(2)}) collective-permute-start(f32[144,128]{1,0:T(8,128)S(1)} %get-tuple-element.54), channel_id=1, source_target_pairs={{2,4},{4,2},{3,5},{5,3},{6,8},{8,6},{7,9},{9,7},{10,12},{12,10},{1... | collective-permute-start | bytes 221192 | tf_op jit(solution)/shard_map/ppermute | solution.py:406
  28.6 0.1 copy.15.lifting_ref
  28.8 0.1 copy.13.solver_ref
  28.8 0.0 copy-start.3
  28.8 0.7 copy-done.3
  29.5 1.5 %own_first.1 = (f32[9,40,128]{2,1,0:T(8,128)S(1)}, f32[144,512]{1,0:T(8,128)S(1)}, bf16[184,128]{1,0:T(8,128)(2,1)S(1)}, bf16[40,192]{1,0:T(8,128)(2,1)S(1)}, bf...) custom-call(f32[9,40,128]{2,1,0:T(8,128)S(1)} %get-tuple-element.56.state_ref, ...), custom_call_target="tpu_custom_call" | custom-call | flops 1000000000 | bytes 10000000 | tf_op jit(solution)/shard_map/own_first/pallas_call | solution.py:355
  31.0 3.4 %step.3 = (f32[9,40,128]{2,1,0:T(8,128)S(1)}, f32[144,512]{1,0:T(8,128)S(1)}, f32[9,40,128]{2,1,0:T(8,128)S(1)}, bf16[288,512]{1,0:T(8,128)(2,1)S(1)}, f32[144,128]{1,0:T(8,128)S(1)}, /*index=5*/f32[144,128]{1,0:T(8,128)S(1)}) custom-call(f32[144,128]{1,0:T(8,128)S(1)} %collective-permute-done.first_ref, f32[144,128]{1,0:T(8,128)S(1)} %collective-permute-done.1.second_ref, ...), custom_call_target="tpu_custom_call" | custom-call | flops 1000000000 | bytes 10000000 | tf_op jit(solution)/shard_map/step/pallas_call | solution.py:355
  34.5 1.9 %all-gather.1 = f32[288,128]{1,0:T(8,128)S(1)} all-gather(f32[144,128]{1,0:T(8,128)S(1)} %get-tuple-element.67), channel_id=3, replica_groups={{0,1},{2,3},{4,5},{6,7},{8,9},{10,11},{12,13},{14,15},{16,17},{18,19},{..., dimensions={0}, use_global_device_ids=true | all-gather | bytes 221184 | tf_op jit(solution)/shard_map/all_gather | solution.py:402
  36.4 8.1 %collective-permute-start.2 = (f32[144,128]{1,0:T(8,128)S(1)}, f32[144,128]{1,0:T(8,128)S(1)}, u32[]{:S(2)}, u32[]{:S(2)}) collective-permute-start(f32[144,128]{1,0:T(8,128)S(1)} %get-tuple-element.69), channel_id=1, source_target_pairs={{2,4},{4,2},{3,5},{5,3},{6,8},{8,6},{7,9},{9,7},{10,12},{12,10},{1... | collective-permute-start | bytes 221192 | tf_op jit(solution)/shard_map/ppermute | solution.py:406
  44.5 1.9 %collective-permute-start.3 = (f32[144,128]{1,0:T(8,128)S(1)}, f32[144,128]{1,0:T(8,128)S(1)}, u32[]{:S(2)}, u32[]{:S(2)}) collective-permute-start(f32[144,128]{1,0:T(8,128)S(1)} %get-tuple-element.70), channel_id=1, source_target_pairs={{0,2},{2,0},{1,3},{3,1},{4,6},{6,4},{5,7},{7,5},{8,10},{10,8},{9,1... | collective-permute-start | bytes 221192 | tf_op jit(solution)/shard_map/ppermute | solution.py:407
  46.4 1.1 %own.3 = (f32[9,40,128]{2,1,0:T(8,128)S(1)}, f32[144,512]{1,0:T(8,128)S(1)}) custom-call(f32[9,40,128]{2,1,0:T(8,128)S(1)} %get-tuple-element.71.state_ref, f32[9,40,128]{2,1,0:T(8,128)S(1)} %get-tuple-element.72.own_ref, bf16[288,512]{1,0:T(8,128)(2,1)S(1)} %get-tuple-element.73.table_ref, f32[144,512]{1,0:T(8,128)S(1)} %get-tuple-element.74.sum_ref, ...), custom_call_target="tpu_custom_call" | custom-call | flops 1000000000 | bytes 10000000 | tf_op jit(solution)/shard_map/own/pallas_call | solution.py:355
  47.5 3.2 %collective-permute-done.3.second_ref = f32[144,128]{1,0:T(8,128)S(1)} collective-permute-done((f32[144,128]{1,0:T(8,128)S(1)}, f32[144,128]{1,0:T(8,128)S(1)}, u32[]{:S(2)}, u32[]{:S(2)}) %collective-permute-start.3) | collective-permute-done | bytes 73760 | tf_op jit(solution)/shard_map/ppermute | solution.py:407
  50.7 3.4 %step.4 = (f32[9,40,128]{2,1,0:T(8,128)S(1)}, f32[144,512]{1,0:T(8,128)S(1)}, f32[9,40,128]{2,1,0:T(8,128)S(1)}, bf16[288,512]{1,0:T(8,128)(2,1)S(1)}, f32[144,128]{1,0:T(8,128)S(1)}, /*index=5*/f32[144,128]{1,0:T(8,128)S(1)}) custom-call(f32[144,128]{1,0:T(8,128)S(1)} %collective-permute-done.2.first_ref, f32[144,128]{1,0:T(8,128)S(1)} %collective-permute-done.3.second_ref, ...), custom_call_target="tpu_custom_call" | custom-call | flops 1000000000 | bytes 10000000 | tf_op jit(solution)/shard_map/step/pallas_call | solution.py:355
  54.2 1.9 %all-gather.2 = f32[288,128]{1,0:T(8,128)S(1)} all-gather(f32[144,128]{1,0:T(8,128)S(1)} %get-tuple-element.79), channel_id=4, replica_groups={{0,1},{2,3},{4,5},{6,7},{8,9},{10,11},{12,13},{14,15},{16,17},{18,19},{..., dimensions={0}, use_global_device_ids=true | all-gather | bytes 221184 | tf_op jit(solution)/shard_map/all_gather | solution.py:402
  56.1 4.2 %collective-permute-start.4 = (f32[144,128]{1,0:T(8,128)S(1)}, f32[144,128]{1,0:T(8,128)S(1)}, u32[]{:S(2)}, u32[]{:S(2)}) collective-permute-start(f32[144,128]{1,0:T(8,128)S(1)} %get-tuple-element.81), channel_id=1, source_target_pairs={{2,4},{4,2},{3,5},{5,3},{6,8},{8,6},{7,9},{9,7},{10,12},{12,10},{1... | collective-permute-start | bytes 221192 | tf_op jit(solution)/shard_map/ppermute | solution.py:406
  60.3 1.9 %collective-permute-start.5 = (f32[144,128]{1,0:T(8,128)S(1)}, f32[144,128]{1,0:T(8,128)S(1)}, u32[]{:S(2)}, u32[]{:S(2)}) collective-permute-start(f32[144,128]{1,0:T(8,128)S(1)} %get-tuple-element.82), channel_id=1, source_target_pairs={{0,2},{2,0},{1,3},{3,1},{4,6},{6,4},{5,7},{7,5},{8,10},{10,8},{9,1... | collective-permute-start | bytes 221192 | tf_op jit(solution)/shard_map/ppermute | solution.py:407
  62.3 1.1 %own.4 = (f32[9,40,128]{2,1,0:T(8,128)S(1)}, f32[144,512]{1,0:T(8,128)S(1)}) custom-call(f32[9,40,128]{2,1,0:T(8,128)S(1)} %get-tuple-element.83.state_ref, f32[9,40,128]{2,1,0:T(8,128)S(1)} %get-tuple-element.84.own_ref, bf16[288,512]{1,0:T(8,128)(2,1)S(1)} %get-tuple-element.85.table_ref, f32[144,512]{1,0:T(8,128)S(1)} %get-tuple-element.86.sum_ref, ...), custom_call_target="tpu_custom_call" | custom-call | flops 1000000000 | bytes 10000000 | tf_op jit(solution)/shard_map/own/pallas_call | solution.py:355
  63.3 3.2 %collective-permute-done.5.second_ref = f32[144,128]{1,0:T(8,128)S(1)} collective-permute-done((f32[144,128]{1,0:T(8,128)S(1)}, f32[144,128]{1,0:T(8,128)S(1)}, u32[]{:S(2)}, u32[]{:S(2)}) %collective-permute-start.5) | collective-permute-done | bytes 73760 | tf_op jit(solution)/shard_map/ppermute | solution.py:407
  66.6 3.4 %step.5 = (f32[9,40,128]{2,1,0:T(8,128)S(1)}, f32[144,512]{1,0:T(8,128)S(1)}, f32[9,40,128]{2,1,0:T(8,128)S(1)}, bf16[288,512]{1,0:T(8,128)(2,1)S(1)}, f32[144,128]{1,0:T(8,128)S(1)}, /*index=5*/f32[144,128]{1,0:T(8,128)S(1)}) custom-call(f32[144,128]{1,0:T(8,128)S(1)} %collective-permute-done.4.first_ref, f32[144,128]{1,0:T(8,128)S(1)} %collective-permute-done.5.second_ref, ...), custom_call_target="tpu_custom_call" | custom-call | flops 1000000000 | bytes 10000000 | tf_op jit(solution)/shard_map/step/pallas_call | solution.py:355
  70.0 1.9 %all-gather.3 = f32[288,128]{1,0:T(8,128)S(1)} all-gather(f32[144,128]{1,0:T(8,128)S(1)} %get-tuple-element.89), channel_id=5, replica_groups={{0,1},{2,3},{4,5},{6,7},{8,9},{10,11},{12,13},{14,15},{16,17},{18,19},{..., dimensions={0}, use_global_device_ids=true | all-gather | bytes 221184 | tf_op jit(solution)/shard_map/all_gather | solution.py:402
  72.0 5.9 %collective-permute-start.6 = (f32[144,128]{1,0:T(8,128)S(1)}, f32[144,128]{1,0:T(8,128)S(1)}, u32[]{:S(2)}, u32[]{:S(2)}) collective-permute-start(f32[144,128]{1,0:T(8,128)S(1)} %get-tuple-element.91), channel_id=1, source_target_pairs={{2,4},{4,2},{3,5},{5,3},{6,8},{8,6},{7,9},{9,7},{10,12},{12,10},{1... | collective-permute-start | bytes 221192 | tf_op jit(solution)/shard_map/ppermute | solution.py:406
  77.8 1.9 %collective-permute-start.7 = (f32[144,128]{1,0:T(8,128)S(1)}, f32[144,128]{1,0:T(8,128)S(1)}, u32[]{:S(2)}, u32[]{:S(2)}) collective-permute-start(f32[144,128]{1,0:T(8,128)S(1)} %get-tuple-element.92), channel_id=1, source_target_pairs={{0,2},{2,0},{1,3},{3,1},{4,6},{6,4},{5,7},{7,5},{8,10},{10,8},{9,1... | collective-permute-start | bytes 221192 | tf_op jit(solution)/shard_map/ppermute | solution.py:407
  79.8 1.1 %own.5 = (f32[9,40,128]{2,1,0:T(8,128)S(1)}, f32[144,512]{1,0:T(8,128)S(1)}) custom-call(f32[9,40,128]{2,1,0:T(8,128)S(1)} %get-tuple-element.93.state_ref, f32[9,40,128]{2,1,0:T(8,128)S(1)} %get-tuple-element.94.own_ref, bf16[288,512]{1,0:T(8,128)(2,1)S(1)} %get-tuple-element.95.table_ref, f32[144,512]{1,0:T(8,128)S(1)} %get-tuple-element.96.sum_ref, ...), custom_call_target="tpu_custom_call" | custom-call | flops 1000000000 | bytes 10000000 | tf_op jit(solution)/shard_map/own/pallas_call | solution.py:355
  80.9 3.2 %collective-permute-done.7.second_ref = f32[144,128]{1,0:T(8,128)S(1)} collective-permute-done((f32[144,128]{1,0:T(8,128)S(1)}, f32[144,128]{1,0:T(8,128)S(1)}, u32[]{:S(2)}, u32[]{:S(2)}) %collective-permute-start.7) | collective-permute-done | bytes 73760 | tf_op jit(solution)/shard_map/ppermute | solution.py:407
  84.1 1.3 %end.1 = f32[9,35,128]{2,1,0:T(8,128)} custom-call(f32[144,128]{1,0:T(8,128)S(1)} %collective-permute-done.6.first_ref, f32[144,128]{1,0:T(8,128)S(1)} %collective-permute-done.7.second_ref, f32[2,144,128]{2,1,0:T(8,128)S(1)} %bitcast.11, f32[9,40,128]{2,1,0:T(8,128)S(1)} %get-tuple-element.97.base_ref, f32[144,512]{1,0:T(8,128)S(1)} %get-tuple-element.98.partial_ref, ...), custom_call_target="tpu_custom_call" | custom-call | flops 1000000000 | bytes 10000000 | tf_op jit(solution)/shard_map/end/pallas_call | solution.py:355
  (23 shorter events, 0.1 us)
Async XLA Ops:
  0.8 1.0 %copy-start = (f32[9,35,128]{2,1,0:T(8,128)S(1)}, f32[9,35,128]{2,1,0:T(8,128)}, u32[]{:S(2)}) copy-start(f32[9,35,128]{2,1,0:T(8,128)} %coef_ref.1) | copy-start | bytes 483844
  0.8 1.0 %copy-start.1 = (f32[3,35,35]{2,1,0:T(8,128)S(1)}, f32[3,35,35]{2,1,0:T(8,128)}, u32[]{:S(2)}) copy-start(f32[3,35,35]{2,1,0:T(8,128)} %stiffness_ref.3) | copy-start | bytes 44104
  0.8 1.0 %copy-start.2 = (s32[4,64]{1,0:T(4,128)S(1)}, s32[4,64]{1,0:T(4,128)}, u32[]{:S(2)}) copy-start(s32[4,64]{1,0:T(4,128)} %faces_ref.1) | copy-start | bytes 3076
  0.8 1.0 %copy-start.4 = (s32[8]{0:T(128)S(1)}, s32[8]{0:T(128)}, u32[]{:S(2)}) copy-start(s32[8]{0:T(128)} %cluster_ref.1) | copy-start | bytes 100
  5.5 23.3 %copy-start.5 = (f32[2,4,9,9,128]{4,1,3,2,0:T(4,128)S(1)}, f32[2,4,9,9,128]{4,1,3,2,0:T(4,128)}, u32[]{:S(2)}) copy-start(f32[2,4,9,9,128]{4,1,3,2,0:T(4,128)} %param.11) | copy-start | bytes 995332
  7.5 21.1 %copy-start.6 = (f32[4,35,15]{1,0,2:T(4,128)S(1)}, f32[4,35,15]{1,0,2:T(4,128)}, u32[]{:S(2)}) copy-start(f32[4,35,15]{1,0,2:T(4,128)} %param.14) | copy-start | bytes 25204
  7.6 23.4 %collective-permute-start.1 = (f32[144,128]{1,0:T(8,128)S(1)}, f32[144,128]{1,0:T(8,128)S(1)}, u32[]{:S(2)}, u32[]{:S(2)}) collective-permute-start(f32[144,128]{1,0:T(8,128)S(1)} %get-tuple-element.55), channel_id=1, source_target_pairs={{0,2},{2,0},{1,3},{3,1},{4,6},{6,4},{5,7},{7,5},{8,10},{10,8},{9,1... | collective-permute-start | bytes 221192 | tf_op jit(solution)/shard_map/ppermute | solution.py:407
  11.1 19.9 %collective-permute-start = (f32[144,128]{1,0:T(8,128)S(1)}, f32[144,128]{1,0:T(8,128)S(1)}, u32[]{:S(2)}, u32[]{:S(2)}) collective-permute-start(f32[144,128]{1,0:T(8,128)S(1)} %get-tuple-element.54), channel_id=1, source_target_pairs={{2,4},{4,2},{3,5},{5,3},{6,8},{8,6},{7,9},{9,7},{10,12},{12,10},{1... | collective-permute-start | bytes 221192 | tf_op jit(solution)/shard_map/ppermute | solution.py:406
  28.8 0.7 copy-start.3
  36.4 14.3 %collective-permute-start.2 = (f32[144,128]{1,0:T(8,128)S(1)}, f32[144,128]{1,0:T(8,128)S(1)}, u32[]{:S(2)}, u32[]{:S(2)}) collective-permute-start(f32[144,128]{1,0:T(8,128)S(1)} %get-tuple-element.69), channel_id=1, source_target_pairs={{2,4},{4,2},{3,5},{5,3},{6,8},{8,6},{7,9},{9,7},{10,12},{12,10},{1... | collective-permute-start | bytes 221192 | tf_op jit(solution)/shard_map/ppermute | solution.py:406
  44.5 6.2 %collective-permute-start.3 = (f32[144,128]{1,0:T(8,128)S(1)}, f32[144,128]{1,0:T(8,128)S(1)}, u32[]{:S(2)}, u32[]{:S(2)}) collective-permute-start(f32[144,128]{1,0:T(8,128)S(1)} %get-tuple-element.70), channel_id=1, source_target_pairs={{0,2},{2,0},{1,3},{3,1},{4,6},{6,4},{5,7},{7,5},{8,10},{10,8},{9,1... | collective-permute-start | bytes 221192 | tf_op jit(solution)/shard_map/ppermute | solution.py:407
  56.1 10.5 %collective-permute-start.4 = (f32[144,128]{1,0:T(8,128)S(1)}, f32[144,128]{1,0:T(8,128)S(1)}, u32[]{:S(2)}, u32[]{:S(2)}) collective-permute-start(f32[144,128]{1,0:T(8,128)S(1)} %get-tuple-element.81), channel_id=1, source_target_pairs={{2,4},{4,2},{3,5},{5,3},{6,8},{8,6},{7,9},{9,7},{10,12},{12,10},{1... | collective-permute-start | bytes 221192 | tf_op jit(solution)/shard_map/ppermute | solution.py:406
  60.3 6.2 %collective-permute-start.5 = (f32[144,128]{1,0:T(8,128)S(1)}, f32[144,128]{1,0:T(8,128)S(1)}, u32[]{:S(2)}, u32[]{:S(2)}) collective-permute-start(f32[144,128]{1,0:T(8,128)S(1)} %get-tuple-element.82), channel_id=1, source_target_pairs={{0,2},{2,0},{1,3},{3,1},{4,6},{6,4},{5,7},{7,5},{8,10},{10,8},{9,1... | collective-permute-start | bytes 221192 | tf_op jit(solution)/shard_map/ppermute | solution.py:407
  72.0 12.1 %collective-permute-start.6 = (f32[144,128]{1,0:T(8,128)S(1)}, f32[144,128]{1,0:T(8,128)S(1)}, u32[]{:S(2)}, u32[]{:S(2)}) collective-permute-start(f32[144,128]{1,0:T(8,128)S(1)} %get-tuple-element.91), channel_id=1, source_target_pairs={{2,4},{4,2},{3,5},{5,3},{6,8},{8,6},{7,9},{9,7},{10,12},{12,10},{1... | collective-permute-start | bytes 221192 | tf_op jit(solution)/shard_map/ppermute | solution.py:406
  77.8 6.2 %collective-permute-start.7 = (f32[144,128]{1,0:T(8,128)S(1)}, f32[144,128]{1,0:T(8,128)S(1)}, u32[]{:S(2)}, u32[]{:S(2)}) collective-permute-start(f32[144,128]{1,0:T(8,128)S(1)} %get-tuple-element.92), channel_id=1, source_target_pairs={{0,2},{2,0},{1,3},{3,1},{4,6},{6,4},{5,7},{7,5},{8,10},{10,8},{9,1... | collective-permute-start | bytes 221192 | tf_op jit(solution)/shard_map/ppermute | solution.py:407
where the time goes:
time: 85.9 us; the launch traced here: 85.4 us
  starting transfers between devices  44.9 us (52%)
  Pallas kernels  20.1 us (23%)
  waiting for transfers between devices  9.73 us (11%)
  blocking collectives  7.78 us (9%)
  local copies, waits for them, and re-layouts  2.63 us (3%)
    ppermute x4, starting transfers between devices, per_device(): first_in = lax.ppermute(first, 'region', outer)  35.6 us
    pallas_call x13, Pallas kernels, call(): pl.pallas_call(kernel, name=name, out_shape=[jax.ShapeDtypeStruct(s, d) f...  20.1 us
    ppermute x4, waiting for transfers between devices, per_device(): second_in = lax.ppermute(second, 'region', inner)  9.71 us
    ppermute x4, starting transfers between devices, per_device(): second_in = lax.ppermute(second, 'region', inner)  9.25 us
    all_gather x4, blocking collectives, per_device(): gathered = lax.all_gather(near_list, 'region', axis_index_groups=cores)  7.78 us
    unnamed x18, local copies, waits for them, and re-layouts  2.62 us
  transfers between devices with their start and end apart: 8, of which 3 were waited for; matrix products, arithmetic and copies ran while one was open for 0% of the time, Pallas kernels for 6%

commit v1 on v0

--- a/solution.py
+++ b/solution.py
@@ -16,7 +16,6 @@
 DERIVS = 5
 TICKS = 4
 LANES = 128
-BLOCK = 16
 STEP = 0.125
 FACTORIALS = (1.0, 2.0, 6.0, 24.0, 120.0)
 F32 = jnp.float32
@@ -64,19 +63,20 @@
 
 
 def contract_star(blocks, base, star_ref, finish):
-    for first in range(0, NQ, 3):
-        totals = [None] * 3
+    for start, size in ((0, 16), (16, 16), (32, 8)):
+        partial = [None] * NQ
         for direction in range(3):
+            row = base + direction * ROWS + start
+            totals = [None] * NQ
             for source in range(NQ):
-                block = blocks[
-                    base + direction * ROWS : base + (direction + 1) * ROWS,
-                    source * LANES : (source + 1) * LANES,
-                ]
-                for k in range(3):
-                    term = block * star_ref[direction, source, first + k : first + k + 1, :]
-                    totals[k] = term if totals[k] is None else totals[k] + term
-        for k in range(3):
-            finish(first + k, totals[k])
+                block = blocks[row : row + size, source * LANES : (source + 1) * LANES]
+                for p in range(NQ):
+                    term = block * star_ref[direction, source, p : p + 1, :]
+                    totals[p] = term if totals[p] is None else totals[p] + term
+            for p in range(NQ):
+                partial[p] = totals[p] if partial[p] is None else partial[p] + totals[p]
+        for p in range(NQ):
+            finish(p, slice(start, start + size), partial[p])
 
 
 def tick_weights(period, tick):
@@ -98,35 +98,34 @@
     return out
 
 
+def weighted(derivs, q, weights):
+    total = derivs[0, q] * weights[0]
+    for k in range(1, DERIVS):
+        total = total + derivs[k, q] * weights[k]
+    return total
+
+
 def predict_and_send(
-    tick, first_state, star_ref, stiff_ref, proj_ref, send_ref, period_ref,
-    table_ref, own_ref, near_list_ref, far_list_ref, derivs, blocks, faces,
+    tick, star_ref, stiff_ref, proj_ref, send_ref, period_ref,
+    derivs, table_ref, near_list_ref, far_list_ref, blocks, faces,
 ):
     def degree(k, carry):
         x = jnp.concatenate([derivs[k, q] for q in range(NQ)], axis=1)
         blocks[...] = matmul(stiff_ref[...], stacked(x, LANES))
 
-        def finish(p, total):
-            derivs[k + 1, p] = total
+        def finish(p, rows, total):
+            derivs[k + 1, p, rows, :] = total
 
         contract_star(blocks, 0, star_ref, finish)
         return carry
 
-    lax.fori_loop(0, DERIVS - 1, degree, 0)
+    for k in range(DERIVS - 1):
+        degree(k, 0)
     period = period_ref[0:1, :]
     now = tick_weights(period, tick)
-    whole = own_weights(period)
     parts = []
     for q in range(NQ):
-        tick_sum = None
-        own_sum = None
-        for k in range(DERIVS):
-            d = derivs[k, q]
-            a, b = d * now[k], d * whole[k]
-            tick_sum = a if tick_sum is None else tick_sum + a
-            own_sum = b if own_sum is None else own_sum + b
-        own_ref[q] = own_sum
-        parts.append(tick_sum)
+        parts.append(weighted(derivs, q, now))
     faces[...] = matmul(proj_ref[...], stacked(jnp.concatenate(parts, axis=1), LANES))
     highs, lows = [], []
     for q in range(NQ):
@@ -148,28 +147,27 @@
 
 def begin_kernel(
     coef_ref, star_ref, stiffness_ref, projection_ref, cluster_ref, faces_ref,
-    state_ref, own_ref, table_ref, near_list_ref, far_list_ref,
+    derivs, table_ref, near_list_ref, far_list_ref,
     stiff_ref, proj_ref, send_ref, period_ref,
-    derivs, blocks, faces, work,
+    blocks, faces, work,
 ):
     lane = lax.broadcasted_iota(jnp.int32, (8, LANES), 1)
     period = jnp.full((8, LANES), 1, jnp.int32)
-    for j in range(LANES // BLOCK):
+    for j in range(LANES // 16):
         c = cluster_ref[j]
         p = jnp.where(c == 0, 1, jnp.where(c == 1, 2, 4))
-        period = jnp.where(lane // BLOCK == j, p, period)
+        period = jnp.where((lane >> 4) == j, p, period)
     period_ref[...] = period
     derivs[0] = jnp.zeros((NQ, ROWS, LANES), F32)
     for q in range(NQ):
         derivs[0, q, 0:BASIS, :] = coef_ref[q]
-    state_ref[...] = derivs[0]
     work[...] = jnp.zeros_like(work)
     for d in range(3):
         weights_into(work, d * ROWS, -stiffness_ref[d], ROWS)
     stiff_ref[...] = work[0 : 3 * ROWS, :].astype(BF16)
     work[...] = jnp.zeros_like(work)
     for f in range(FACES):
-        weights_into(work, f * FACE_ROWS, projection_ref[f], ROWS)
+        weights_into(work, f * FACE_ROWS, projection_ref[:, f, :], ROWS)
     proj_ref[...] = work[0 : FACES * FACE_ROWS, :].astype(BF16)
     column = lax.broadcasted_iota(jnp.int32, (FACES * LANES, LANES), 0)
     near = jnp.concatenate([faces_ref[3:4, :], faces_ref[0:1, :]], axis=1)
@@ -177,8 +175,8 @@
     send_ref[:, :LANES] = (column == near).astype(F32).astype(BF16)
     send_ref[:, LANES:] = (column == far).astype(F32).astype(BF16)
     predict_and_send(
-        0, None, star_ref, stiff_ref, proj_ref, send_ref, period_ref,
-        table_ref, own_ref, near_list_ref, far_list_ref, derivs, blocks, faces,
+        0, star_ref, stiff_ref, proj_ref, send_ref, period_ref,
+        derivs, table_ref, near_list_ref, far_list_ref, blocks, faces,
     )
 
 
@@ -208,39 +206,51 @@
 
 
 def ending_mask(period, tick):
-    return lax.rem(jnp.full_like(period, tick + 1), period) == 0
+    return period <= ((tick + 1) & -(tick + 1))
 
 
 def own_body(
-    tick, state_ref, own_ref, table_ref, sum_ref, star_ref, solver_ref, period_ref,
+    tick, derivs, table_ref, sum_ref, star_ref, solver_ref, period_ref,
     both_ref, lift_ref, local_ref, base_ref, partial_ref, big, flux,
 ):
-    ending = ending_mask(period_ref[0:1, :], tick)
-    big[...] = matmul(both_ref[...], stacked(wide(own_ref), LANES))
+    period = period_ref[0:1, :]
+    ending = ending_mask(period, tick)
+    whole = own_weights(period)
+    own = jnp.concatenate([weighted(derivs, q, whole) for q in range(NQ)], axis=1)
+    big[...] = matmul(both_ref[...], stacked(own, LANES))
     face_contract(
         lambda q, f: big[f * FACE_ROWS : (f + 1) * FACE_ROWS, q * LANES : (q + 1) * LANES],
         solver_ref, 0, flux,
     )
     lifted = matmul(lift_ref[...], stacked(flux[...], 192))
-    def finish(p, total):
-        change = total - lifted[:, p * LANES : (p + 1) * LANES]
-        base_ref[p] = state_ref[p] + jnp.where(ending, change, 0.0)
+    for p in range(NQ):
+        base_ref[p] = lifted[:, p * LANES : (p + 1) * LANES]
+
+    def finish(p, rows, total):
+        change = total - base_ref[p, rows, :]
+        base_ref[p, rows, :] = derivs[0, p, rows, :] + jnp.where(ending, change, 0.0)
 
     contract_star(big, FACES * FACE_ROWS, star_ref, finish)
     both = matmul(table_ref[...], local_ref[...])
     picked = both[:TABLE] + both[TABLE:]
-    partial_ref[...] = picked if sum_ref is None else sum_ref[...] + picked
+    if sum_ref is None:
+        partial_ref[...] = picked
+    else:
+        cleared = ending_mask(period, tick - 1)
+        for f in range(FACES):
+            where = slice(f * LANES, (f + 1) * LANES)
+            partial_ref[:, where] = picked[:, where] + jnp.where(cleared, 0.0, sum_ref[:, where])
 
 
 def own_first_kernel(
-    state_ref, own_ref, table_ref, star_ref, solver_ref, period_ref,
+    derivs, table_ref, star_ref, solver_ref, period_ref,
     stiffness_ref, projection_ref, lifting_ref, neighbor_ref, order_ref,
     base_ref, partial_ref, both_ref, lift_ref, local_ref, remote_ref,
     big, flux, work, work_lift,
 ):
     work[...] = jnp.zeros_like(work)
     for f in range(FACES):
-        weights_into(work, f * FACE_ROWS, projection_ref[f], ROWS)
+        weights_into(work, f * FACE_ROWS, projection_ref[:, f, :], ROWS)
     for d in range(3):
         weights_into(work, FACES * FACE_ROWS + d * ROWS, stiffness_ref[d].T, ROWS)
     both_ref[...] = work[...].astype(BF16)
@@ -263,18 +273,18 @@
                 start = (g - FACES) * LANES
                 remote_ref[start : start + LANES, f * LANES : (f + 1) * LANES] = chosen
     own_body(
-        0, state_ref, own_ref, table_ref, None, star_ref, solver_ref, period_ref,
+        0, derivs, table_ref, None, star_ref, solver_ref, period_ref,
         both_ref, lift_ref, local_ref, base_ref, partial_ref, big, flux,
     )
 
 
 def own_kernel(
-    tick, state_ref, own_ref, table_ref, sum_ref, star_ref, solver_ref, period_ref,
+    tick, derivs, table_ref, sum_ref, star_ref, solver_ref, period_ref,
     both_ref, lift_ref, local_ref, order_ref,
     base_ref, partial_ref, big, flux,
 ):
     own_body(
-        tick, state_ref, own_ref, table_ref, sum_ref, star_ref, solver_ref, period_ref,
+        tick, derivs, table_ref, sum_ref, star_ref, solver_ref, period_ref,
         both_ref, lift_ref, local_ref, base_ref, partial_ref, big, flux,
     )
 
@@ -309,8 +319,8 @@
 def step_kernel(
     tick, first_ref, second_ref, gathered_ref, base_ref, partial_ref, star_ref, solver_ref,
     period_ref, lift_ref, remote_ref, stiff_ref, proj_ref, send_ref,
-    state_ref, sum_ref, own_ref, table_ref, near_list_ref, far_list_ref,
-    sums, flux, derivs, blocks, faces,
+    derivs, sums, table_ref, near_list_ref, far_list_ref,
+    flux, blocks, faces,
 ):
     lifted = near_body(
         tick, first_ref, second_ref, gathered_ref, base_ref, partial_ref, solver_ref, period_ref,
@@ -321,13 +331,9 @@
         change = jnp.where(ending, lifted[:, p * LANES : (p + 1) * LANES], 0.0)
         value = base_ref[p] - change
         derivs[0, p] = value
-        state_ref[p] = value
-    for f in range(FACES):
-        part = sums[:, f * LANES : (f + 1) * LANES]
-        sum_ref[:, f * LANES : (f + 1) * LANES] = jnp.where(ending, 0.0, part)
     predict_and_send(
-        tick + 1, None, star_ref, stiff_ref, proj_ref, send_ref, period_ref,
-        table_ref, own_ref, near_list_ref, far_list_ref, derivs, blocks, faces,
+        tick + 1, star_ref, stiff_ref, proj_ref, send_ref, period_ref,
+        derivs, table_ref, near_list_ref, far_list_ref, blocks, faces,
     )
 
 
@@ -378,6 +384,7 @@
 def per_device(
     coefficients, star, solvers, stiffness, projection, lifting, block_cluster, neighbors, send_faces
 ):
+    projection = jnp.transpose(projection, (1, 0, 2))
     count = lax.axis_size("region")
     cores = [[2 * k, 2 * k + 1] for k in range(count // 2)]
     pairs = ([], [])
@@ -385,15 +392,15 @@
         pairs[(i // 2) % 2] .extend([(i, i + 2), (i + 2, i)])
     inner, outer = pairs
 
-    (state, own, table, near_list, far_list, stiff_w, proj_w, send_w, period) = call(
+    (derivs, table, near_list, far_list, stiff_w, proj_w, send_w, period) = call(
         begin_kernel, "begin",
         (coefficients, star, stiffness, projection, block_cluster, send_faces),
         (
-            STATE, STATE, PAIRED, LIST, LIST,
+            DERIV, PAIRED, LIST, LIST,
             ((3 * ROWS, LANES), BF16), ((FACES * FACE_ROWS, LANES), BF16),
             ((FACES * LANES, 2 * LANES), BF16), ((8, LANES), jnp.int32),
         ),
-        (DERIV, BLOCKS, FACE, ((3 * ROWS, LANES), F32)),
+        (BLOCKS, FACE, ((3 * ROWS, LANES), F32)),
         10**9,
         [VMEM, VMEM, VMEM, VMEM, SMEM, VMEM],
     )
@@ -409,7 +416,7 @@
             base, partial, both_w, lift_w, local_w, remote_w = call(
                 own_first_kernel, "own_first",
                 (
-                    state, own, table, star, solvers, period,
+                    derivs, table, star, solvers, period,
                     stiffness, projection, lifting, neighbors, first[:8],
                 ),
                 (
@@ -422,18 +429,18 @@
         else:
             base, partial = call(
                 functools.partial(own_kernel, tick), "own",
-                (state, own, table, sums, star, solvers, period, both_w, lift_w, local_w, first[:8]),
+                (derivs, table, sums, star, solvers, period, both_w, lift_w, local_w, first[:8]),
                 (STATE, SUMS), (BIG, FACE), 10**9,
             )
         if tick < TICKS - 1:
-            state, sums, own, table, near_list, far_list = call(
+            derivs, sums, table, near_list, far_list = call(
                 functools.partial(step_kernel, tick), "step",
                 (
                     first_in, second_in, gathered, base, partial, star, solvers,
                     period, lift_w, remote_w, stiff_w, proj_w, send_w,
                 ),
-                (STATE, SUMS, STATE, PAIRED, LIST, LIST),
-                (SUMS, FACE, DERIV, BLOCKS, FACE), 10**9,
+                (DERIV, SUMS, PAIRED, LIST, LIST),
+                (FACE, BLOCKS, FACE), 10**9,
             )
     (updated,) = call(
         end_kernel, "end",

time: 85.9 us -> 83.5 us (0.972)
  Pallas kernels: 20.1 us -> 17.9 us
    pallas_call x13, Pallas kernels: 20.1 us -> 17.9 us  [call(): pl.pallas_call(kernel, name=name, out_shape=[jax.ShapeDtypeStruct(s, d) f...]
    unnamed x18 -> x19, local copies, waits for them, and re-layouts: 2.62 us -> 2.51 us
where the time goes in v1:
time: 83.5 us; the launch traced here: 83.1 us
  starting transfers between devices  45 us (54%)
  Pallas kernels  17.9 us (21%)
  waiting for transfers between devices  9.55 us (11%)
  blocking collectives  7.78 us (9%)
  local copies, waits for them, and re-layouts  2.52 us (3%)
    ppermute x4, starting transfers between devices, per_device(): first_in = lax.ppermute(first, 'region', outer)  35.6 us
    pallas_call x13, Pallas kernels, call(): pl.pallas_call(kernel, name=name, out_shape=[jax.ShapeDtypeStruct(s, d) f...  17.9 us
    ppermute x4, waiting for transfers between devices, per_device(): second_in = lax.ppermute(second, 'region', inner)  9.53 us
    ppermute x4, starting transfers between devices, per_device(): second_in = lax.ppermute(second, 'region', inner)  9.43 us
    all_gather x4, blocking collectives, per_device(): gathered = lax.all_gather(near_list, 'region', axis_index_groups=cores)  7.78 us
    unnamed x19, local copies, waits for them, and re-layouts  2.51 us
  transfers between devices with their start and end apart: 8, of which 3 were waited for; matrix products, arithmetic and copies ran while one was open for 0% of the time, Pallas kernels for 6%

profile of v1, /device:TPU:6, one launch (start us, length us, event | category | flops | bytes accessed | tf_op | source)
XLA Modules:
  0.0 83.1 jit_solution(14254374702652709475)
XLA Ops:
  0.0 1.0 %copy.10.star_ref = f32[3,9,9,128]{3,2,1,0:T(8,128)S(1)} copy(f32[3,9,9,128]{3,0,2,1:T(4,128)} %param.10) | data formatting | bytes 248832 | tf_op args[1]
  1.0 0.0 copy-start.5
  1.1 0.0 copy-done
  1.1 0.6 copy-done.5
  1.7 3.1 %begin.1 = (f32[5,9,40,128]{3,2,1,0:T(8,128)S(1)}, bf16[288,512]{1,0:T(8,128)(2,1)S(1)}, f32[144,128]{1,0:T(8,128)S(1)}, f32[144,128]{1,0:T(8,128)S(1)}, bf16[12...) custom-call(f32[9,35,128]{2,1,0:T(8,128)S(1)} %copy-done, ...), custom_call_target="tpu_custom_call" | custom-call | flops 1000000000 | bytes 10000000 | tf_op jit(solution)/shard_map/begin/pallas_call | solution.py:361
  4.8 2.0 %all-gather = f32[288,128]{1,0:T(8,128)S(1)} all-gather(f32[144,128]{1,0:T(8,128)S(1)} %get-tuple-element.48), channel_id=2, replica_groups={{0,1},{2,3},{4,5},{6,7},{8,9},{10,11},{12,13},{14,15},{16,17},{18,19},{..., dimensions={0}, use_global_device_ids=true | all-gather | bytes 221184 | tf_op jit(solution)/shard_map/all_gather | solution.py:409
  6.8 3.5 %collective-permute-start.1 = (f32[144,128]{1,0:T(8,128)S(1)}, f32[144,128]{1,0:T(8,128)S(1)}, u32[]{:S(2)}, u32[]{:S(2)}) collective-permute-start(f32[144,128]{1,0:T(8,128)S(1)} %get-tuple-element.51), channel_id=1, source_target_pairs={{0,2},{2,0},{1,3},{3,1},{4,6},{6,4},{5,7},{7,5},{8,10},{10,8},{9,1... | collective-permute-start | bytes 221192 | tf_op jit(solution)/shard_map/ppermute | solution.py:414
  10.3 17.5 %collective-permute-start = (f32[144,128]{1,0:T(8,128)S(1)}, f32[144,128]{1,0:T(8,128)S(1)}, u32[]{:S(2)}, u32[]{:S(2)}) collective-permute-start(f32[144,128]{1,0:T(8,128)S(1)} %get-tuple-element.50), channel_id=1, source_target_pairs={{2,4},{4,2},{3,5},{5,3},{6,8},{8,6},{7,9},{9,7},{10,12},{12,10},{1... | collective-permute-start | bytes 221192 | tf_op jit(solution)/shard_map/ppermute | solution.py:413
  27.9 0.1 copy.13.lifting_ref
  28.0 0.1 copy.12.solver_ref
  28.1 0.7 copy-done.4
  28.8 1.5 %own_first.1 = (f32[9,40,128]{2,1,0:T(8,128)S(1)}, f32[144,512]{1,0:T(8,128)S(1)}, bf16[184,128]{1,0:T(8,128)(2,1)S(1)}, bf16[40,192]{1,0:T(8,128)(2,1)S(1)}, bf...) custom-call(f32[5,9,40,128]{3,2,1,0:T(8,128)S(1)} %get-tuple-element.52.derivs, ...), custom_call_target="tpu_custom_call" | custom-call | flops 1000000000 | bytes 10000000 | tf_op jit(solution)/shard_map/own_first/pallas_call | solution.py:361
  30.3 2.9 %step.3 = (f32[5,9,40,128]{3,2,1,0:T(8,128)S(1)}, f32[144,512]{1,0:T(8,128)S(1)}, bf16[288,512]{1,0:T(8,128)(2,1)S(1)}, f32[144,128]{1,0:T(8,128)S(1)}, f32[144,128]{1,0:T(8,128)S(1)}) custom-call(f32[144,128]{1,0:T(8,128)S(1)} %collective-permute-done.first_ref, f32[144,128]{1,0:T(8,128)S(1)} %collective-permute-done.1.second_ref, ...), custom_call_target="tpu_custom_call" | custom-call | flops 1000000000 | bytes 10000000 | tf_op jit(solution)/shard_map/step/pallas_call | solution.py:361
  33.2 1.9 %all-gather.1 = f32[288,128]{1,0:T(8,128)S(1)} all-gather(f32[144,128]{1,0:T(8,128)S(1)} %get-tuple-element.62), channel_id=3, replica_groups={{0,1},{2,3},{4,5},{6,7},{8,9},{10,11},{12,13},{14,15},{16,17},{18,19},{..., dimensions={0}, use_global_device_ids=true | all-gather | bytes 221184 | tf_op jit(solution)/shard_map/all_gather | solution.py:409
  35.2 8.0 %collective-permute-start.2 = (f32[144,128]{1,0:T(8,128)S(1)}, f32[144,128]{1,0:T(8,128)S(1)}, u32[]{:S(2)}, u32[]{:S(2)}) collective-permute-start(f32[144,128]{1,0:T(8,128)S(1)} %get-tuple-element.64), channel_id=1, source_target_pairs={{2,4},{4,2},{3,5},{5,3},{6,8},{8,6},{7,9},{9,7},{10,12},{12,10},{1... | collective-permute-start | bytes 221192 | tf_op jit(solution)/shard_map/ppermute | solution.py:413
  43.2 1.9 %collective-permute-start.3 = (f32[144,128]{1,0:T(8,128)S(1)}, f32[144,128]{1,0:T(8,128)S(1)}, u32[]{:S(2)}, u32[]{:S(2)}) collective-permute-start(f32[144,128]{1,0:T(8,128)S(1)} %get-tuple-element.65), channel_id=1, source_target_pairs={{0,2},{2,0},{1,3},{3,1},{4,6},{6,4},{5,7},{7,5},{8,10},{10,8},{9,1... | collective-permute-start | bytes 221192 | tf_op jit(solution)/shard_map/ppermute | solution.py:414
  45.1 1.1 %own.3 = (f32[9,40,128]{2,1,0:T(8,128)S(1)}, f32[144,512]{1,0:T(8,128)S(1)}) custom-call(f32[5,9,40,128]{3,2,1,0:T(8,128)S(1)} %get-tuple-element.66.derivs, bf16[288,512]{1,0:T(8,128)(2,1)S(1)} %get-tuple-element.67.table_ref, f32[144,512]{1,0:T(8,128)S(1)} %get-tuple-element.68.sum_ref, f32[3,9,9,128]{3,2,1,0:T(8,128)S(1)} %copy.10.star_ref, ...), custom_call_target="tpu_custom_call" | custom-call | flops 1000000000 | bytes 10000000 | tf_op jit(solution)/shard_map/own/pallas_call | solution.py:361
  46.2 3.2 %collective-permute-done.3.second_ref = f32[144,128]{1,0:T(8,128)S(1)} collective-permute-done((f32[144,128]{1,0:T(8,128)S(1)}, f32[144,128]{1,0:T(8,128)S(1)}, u32[]{:S(2)}, u32[]{:S(2)}) %collective-permute-start.3) | collective-permute-done | bytes 73760 | tf_op jit(solution)/shard_map/ppermute | solution.py:414
  49.5 2.9 %step.4 = (f32[5,9,40,128]{3,2,1,0:T(8,128)S(1)}, f32[144,512]{1,0:T(8,128)S(1)}, bf16[288,512]{1,0:T(8,128)(2,1)S(1)}, f32[144,128]{1,0:T(8,128)S(1)}, f32[144,128]{1,0:T(8,128)S(1)}) custom-call(f32[144,128]{1,0:T(8,128)S(1)} %collective-permute-done.2.first_ref, f32[144,128]{1,0:T(8,128)S(1)} %collective-permute-done.3.second_ref, ...), custom_call_target="tpu_custom_call" | custom-call | flops 1000000000 | bytes 10000000 | tf_op jit(solution)/shard_map/step/pallas_call | solution.py:361
  52.4 1.9 %all-gather.2 = f32[288,128]{1,0:T(8,128)S(1)} all-gather(f32[144,128]{1,0:T(8,128)S(1)} %get-tuple-element.73), channel_id=4, replica_groups={{0,1},{2,3},{4,5},{6,7},{8,9},{10,11},{12,13},{14,15},{16,17},{18,19},{..., dimensions={0}, use_global_device_ids=true | all-gather | bytes 221184 | tf_op jit(solution)/shard_map/all_gather | solution.py:409
  54.4 4.2 %collective-permute-start.4 = (f32[144,128]{1,0:T(8,128)S(1)}, f32[144,128]{1,0:T(8,128)S(1)}, u32[]{:S(2)}, u32[]{:S(2)}) collective-permute-start(f32[144,128]{1,0:T(8,128)S(1)} %get-tuple-element.75), channel_id=1, source_target_pairs={{2,4},{4,2},{3,5},{5,3},{6,8},{8,6},{7,9},{9,7},{10,12},{12,10},{1... | collective-permute-start | bytes 221192 | tf_op jit(solution)/shard_map/ppermute | solution.py:413
  58.6 2.1 %collective-permute-start.5 = (f32[144,128]{1,0:T(8,128)S(1)}, f32[144,128]{1,0:T(8,128)S(1)}, u32[]{:S(2)}, u32[]{:S(2)}) collective-permute-start(f32[144,128]{1,0:T(8,128)S(1)} %get-tuple-element.76), channel_id=1, source_target_pairs={{0,2},{2,0},{1,3},{3,1},{4,6},{6,4},{5,7},{7,5},{8,10},{10,8},{9,1... | collective-permute-start | bytes 221192 | tf_op jit(solution)/shard_map/ppermute | solution.py:414
  60.7 1.1 %own.4 = (f32[9,40,128]{2,1,0:T(8,128)S(1)}, f32[144,512]{1,0:T(8,128)S(1)}) custom-call(f32[5,9,40,128]{3,2,1,0:T(8,128)S(1)} %get-tuple-element.77.derivs, bf16[288,512]{1,0:T(8,128)(2,1)S(1)} %get-tuple-element.78.table_ref, f32[144,512]{1,0:T(8,128)S(1)} %get-tuple-element.79.sum_ref, f32[3,9,9,128]{3,2,1,0:T(8,128)S(1)} %copy.10.star_ref, ...), custom_call_target="tpu_custom_call" | custom-call | flops 1000000000 | bytes 10000000 | tf_op jit(solution)/shard_map/own/pallas_call | solution.py:361
  61.8 3.1 %collective-permute-done.5.second_ref = f32[144,128]{1,0:T(8,128)S(1)} collective-permute-done((f32[144,128]{1,0:T(8,128)S(1)}, f32[144,128]{1,0:T(8,128)S(1)}, u32[]{:S(2)}, u32[]{:S(2)}) %collective-permute-start.5) | collective-permute-done | bytes 73760 | tf_op jit(solution)/shard_map/ppermute | solution.py:414
  64.8 0.0 collective-permute-done.4.first_ref
  64.8 2.9 %step.5 = (f32[5,9,40,128]{3,2,1,0:T(8,128)S(1)}, f32[144,512]{1,0:T(8,128)S(1)}, bf16[288,512]{1,0:T(8,128)(2,1)S(1)}, f32[144,128]{1,0:T(8,128)S(1)}, f32[144,128]{1,0:T(8,128)S(1)}) custom-call(f32[144,128]{1,0:T(8,128)S(1)} %collective-permute-done.4.first_ref, f32[144,128]{1,0:T(8,128)S(1)} %collective-permute-done.5.second_ref, ...), custom_call_target="tpu_custom_call" | custom-call | flops 1000000000 | bytes 10000000 | tf_op jit(solution)/shard_map/step/pallas_call | solution.py:361
  67.8 1.9 %all-gather.3 = f32[288,128]{1,0:T(8,128)S(1)} all-gather(f32[144,128]{1,0:T(8,128)S(1)} %get-tuple-element.82), channel_id=5, replica_groups={{0,1},{2,3},{4,5},{6,7},{8,9},{10,11},{12,13},{14,15},{16,17},{18,19},{..., dimensions={0}, use_global_device_ids=true | all-gather | bytes 221184 | tf_op jit(solution)/shard_map/all_gather | solution.py:409
  69.7 5.9 %collective-permute-start.6 = (f32[144,128]{1,0:T(8,128)S(1)}, f32[144,128]{1,0:T(8,128)S(1)}, u32[]{:S(2)}, u32[]{:S(2)}) collective-permute-start(f32[144,128]{1,0:T(8,128)S(1)} %get-tuple-element.84), channel_id=1, source_target_pairs={{2,4},{4,2},{3,5},{5,3},{6,8},{8,6},{7,9},{9,7},{10,12},{12,10},{1... | collective-permute-start | bytes 221192 | tf_op jit(solution)/shard_map/ppermute | solution.py:413
  75.6 1.9 %collective-permute-start.7 = (f32[144,128]{1,0:T(8,128)S(1)}, f32[144,128]{1,0:T(8,128)S(1)}, u32[]{:S(2)}, u32[]{:S(2)}) collective-permute-start(f32[144,128]{1,0:T(8,128)S(1)} %get-tuple-element.85), channel_id=1, source_target_pairs={{0,2},{2,0},{1,3},{3,1},{4,6},{6,4},{5,7},{7,5},{8,10},{10,8},{9,1... | collective-permute-start | bytes 221192 | tf_op jit(solution)/shard_map/ppermute | solution.py:414
  77.5 1.1 %own.5 = (f32[9,40,128]{2,1,0:T(8,128)S(1)}, f32[144,512]{1,0:T(8,128)S(1)}) custom-call(f32[5,9,40,128]{3,2,1,0:T(8,128)S(1)} %get-tuple-element.86.derivs, bf16[288,512]{1,0:T(8,128)(2,1)S(1)} %get-tuple-element.87.table_ref, f32[144,512]{1,0:T(8,128)S(1)} %get-tuple-element.88.sum_ref, f32[3,9,9,128]{3,2,1,0:T(8,128)S(1)} %copy.10.star_ref, ...), custom_call_target="tpu_custom_call" | custom-call | flops 1000000000 | bytes 10000000 | tf_op jit(solution)/shard_map/own/pallas_call | solution.py:361
  78.6 3.2 %collective-permute-done.7.second_ref = f32[144,128]{1,0:T(8,128)S(1)} collective-permute-done((f32[144,128]{1,0:T(8,128)S(1)}, f32[144,128]{1,0:T(8,128)S(1)}, u32[]{:S(2)}, u32[]{:S(2)}) %collective-permute-start.7) | collective-permute-done | bytes 73760 | tf_op jit(solution)/shard_map/ppermute | solution.py:414
  81.8 1.3 %end.1 = f32[9,35,128]{2,1,0:T(8,128)} custom-call(f32[144,128]{1,0:T(8,128)S(1)} %collective-permute-done.6.first_ref, f32[144,128]{1,0:T(8,128)S(1)} %collective-permute-done.7.second_ref, f32[2,144,128]{2,1,0:T(8,128)S(1)} %bitcast.10, f32[9,40,128]{2,1,0:T(8,128)S(1)} %get-tuple-element.89.base_ref, f32[144,512]{1,0:T(8,128)S(1)} %get-tuple-element.90.partial_ref, ...), custom_call_target="tpu_custom_call" | custom-call | flops 1000000000 | bytes 10000000 | tf_op jit(solution)/shard_map/end/pallas_call | solution.py:361
  (24 shorter events, 0.1 us)
Async XLA Ops:
  0.0 1.0 %copy-start.1 = (f32[3,35,35]{2,1,0:T(8,128)S(1)}, f32[3,35,35]{2,1,0:T(8,128)}, u32[]{:S(2)}) copy-start(f32[3,35,35]{2,1,0:T(8,128)} %stiffness_ref.3) | copy-start | bytes 44104
  0.0 1.0 %copy-start.3 = (s32[4,64]{1,0:T(4,128)S(1)}, s32[4,64]{1,0:T(4,128)}, u32[]{:S(2)}) copy-start(s32[4,64]{1,0:T(4,128)} %faces_ref.1) | copy-start | bytes 3076
  0.0 1.0 %copy-start.2 = (f32[4,15,35]{2,0,1:T(4,128)S(1)}, f32[4,15,35]{2,0,1:T(4,128)}, u32[]{:S(2)}) copy-start(f32[4,15,35]{2,0,1:T(4,128)} %param.13) | copy-start | bytes 25204
  0.0 1.1 %copy-start = (f32[9,35,128]{2,1,0:T(8,128)S(1)}, f32[9,35,128]{2,1,0:T(8,128)}, u32[]{:S(2)}) copy-start(f32[9,35,128]{2,1,0:T(8,128)} %coef_ref.1) | copy-start | bytes 483844
  1.0 0.7 copy-start.5
  4.8 23.3 %copy-start.6 = (f32[2,4,9,9,128]{4,1,3,2,0:T(4,128)S(1)}, f32[2,4,9,9,128]{4,1,3,2,0:T(4,128)}, u32[]{:S(2)}) copy-start(f32[2,4,9,9,128]{4,1,3,2,0:T(4,128)} %param.11) | copy-start | bytes 995332
  6.8 21.1 %copy-start.7 = (f32[4,35,15]{1,0,2:T(4,128)S(1)}, f32[4,35,15]{1,0,2:T(4,128)}, u32[]{:S(2)}) copy-start(f32[4,35,15]{1,0,2:T(4,128)} %param.14) | copy-start | bytes 25204
  6.8 23.4 %collective-permute-start.1 = (f32[144,128]{1,0:T(8,128)S(1)}, f32[144,128]{1,0:T(8,128)S(1)}, u32[]{:S(2)}, u32[]{:S(2)}) collective-permute-start(f32[144,128]{1,0:T(8,128)S(1)} %get-tuple-element.51), channel_id=1, source_target_pairs={{0,2},{2,0},{1,3},{3,1},{4,6},{6,4},{5,7},{7,5},{8,10},{10,8},{9,1... | collective-permute-start | bytes 221192 | tf_op jit(solution)/shard_map/ppermute | solution.py:414
  10.3 20.0 %collective-permute-start = (f32[144,128]{1,0:T(8,128)S(1)}, f32[144,128]{1,0:T(8,128)S(1)}, u32[]{:S(2)}, u32[]{:S(2)}) collective-permute-start(f32[144,128]{1,0:T(8,128)S(1)} %get-tuple-element.50), channel_id=1, source_target_pairs={{2,4},{4,2},{3,5},{5,3},{6,8},{8,6},{7,9},{9,7},{10,12},{12,10},{1... | collective-permute-start | bytes 221192 | tf_op jit(solution)/shard_map/ppermute | solution.py:413
  28.1 0.7 copy-start.4
  35.2 14.3 %collective-permute-start.2 = (f32[144,128]{1,0:T(8,128)S(1)}, f32[144,128]{1,0:T(8,128)S(1)}, u32[]{:S(2)}, u32[]{:S(2)}) collective-permute-start(f32[144,128]{1,0:T(8,128)S(1)} %get-tuple-element.64), channel_id=1, source_target_pairs={{2,4},{4,2},{3,5},{5,3},{6,8},{8,6},{7,9},{9,7},{10,12},{12,10},{1... | collective-permute-start | bytes 221192 | tf_op jit(solution)/shard_map/ppermute | solution.py:413
  43.2 6.2 %collective-permute-start.3 = (f32[144,128]{1,0:T(8,128)S(1)}, f32[144,128]{1,0:T(8,128)S(1)}, u32[]{:S(2)}, u32[]{:S(2)}) collective-permute-start(f32[144,128]{1,0:T(8,128)S(1)} %get-tuple-element.65), channel_id=1, source_target_pairs={{0,2},{2,0},{1,3},{3,1},{4,6},{6,4},{5,7},{7,5},{8,10},{10,8},{9,1... | collective-permute-start | bytes 221192 | tf_op jit(solution)/shard_map/ppermute | solution.py:414
  54.4 10.5 %collective-permute-start.4 = (f32[144,128]{1,0:T(8,128)S(1)}, f32[144,128]{1,0:T(8,128)S(1)}, u32[]{:S(2)}, u32[]{:S(2)}) collective-permute-start(f32[144,128]{1,0:T(8,128)S(1)} %get-tuple-element.75), channel_id=1, source_target_pairs={{2,4},{4,2},{3,5},{5,3},{6,8},{8,6},{7,9},{9,7},{10,12},{12,10},{1... | collective-permute-start | bytes 221192 | tf_op jit(solution)/shard_map/ppermute | solution.py:413
  58.6 6.2 %collective-permute-start.5 = (f32[144,128]{1,0:T(8,128)S(1)}, f32[144,128]{1,0:T(8,128)S(1)}, u32[]{:S(2)}, u32[]{:S(2)}) collective-permute-start(f32[144,128]{1,0:T(8,128)S(1)} %get-tuple-element.76), channel_id=1, source_target_pairs={{0,2},{2,0},{1,3},{3,1},{4,6},{6,4},{5,7},{7,5},{8,10},{10,8},{9,1... | collective-permute-start | bytes 221192 | tf_op jit(solution)/shard_map/ppermute | solution.py:414
  69.7 12.1 %collective-permute-start.6 = (f32[144,128]{1,0:T(8,128)S(1)}, f32[144,128]{1,0:T(8,128)S(1)}, u32[]{:S(2)}, u32[]{:S(2)}) collective-permute-start(f32[144,128]{1,0:T(8,128)S(1)} %get-tuple-element.84), channel_id=1, source_target_pairs={{2,4},{4,2},{3,5},{5,3},{6,8},{8,6},{7,9},{9,7},{10,12},{12,10},{1... | collective-permute-start | bytes 221192 | tf_op jit(solution)/shard_map/ppermute | solution.py:413
  75.6 6.2 %collective-permute-start.7 = (f32[144,128]{1,0:T(8,128)S(1)}, f32[144,128]{1,0:T(8,128)S(1)}, u32[]{:S(2)}, u32[]{:S(2)}) collective-permute-start(f32[144,128]{1,0:T(8,128)S(1)} %get-tuple-element.85), channel_id=1, source_target_pairs={{0,2},{2,0},{1,3},{3,1},{4,6},{6,4},{5,7},{7,5},{8,10},{10,8},{9,1... | collective-permute-start | bytes 221192 | tf_op jit(solution)/shard_map/ppermute | solution.py:414

commit v2 on v1

--- a/solution.py
+++ b/solution.py
@@ -121,8 +121,10 @@
 
     for k in range(DERIVS - 1):
         degree(k, 0)
-    period = period_ref[0:1, :]
-    now = tick_weights(period, tick)
+    if tick == 0:
+        now = [STEP ** (k + 1) / FACTORIALS[k] for k in range(DERIVS)]
+    else:
+        now = tick_weights(period_ref[0:1, :], tick)
     parts = []
     for q in range(NQ):
         parts.append(weighted(derivs, q, now))
@@ -146,18 +148,11 @@
 
 
 def begin_kernel(
-    coef_ref, star_ref, stiffness_ref, projection_ref, cluster_ref, faces_ref,
+    coef_ref, star_ref, stiffness_ref, projection_ref, faces_ref,
     derivs, table_ref, near_list_ref, far_list_ref,
-    stiff_ref, proj_ref, send_ref, period_ref,
+    stiff_ref, proj_ref, send_ref,
     blocks, faces, work,
 ):
-    lane = lax.broadcasted_iota(jnp.int32, (8, LANES), 1)
-    period = jnp.full((8, LANES), 1, jnp.int32)
-    for j in range(LANES // 16):
-        c = cluster_ref[j]
-        p = jnp.where(c == 0, 1, jnp.where(c == 1, 2, 4))
-        period = jnp.where((lane >> 4) == j, p, period)
-    period_ref[...] = period
     derivs[0] = jnp.zeros((NQ, ROWS, LANES), F32)
     for q in range(NQ):
         derivs[0, q, 0:BASIS, :] = coef_ref[q]
@@ -175,7 +170,7 @@
     send_ref[:, :LANES] = (column == near).astype(F32).astype(BF16)
     send_ref[:, LANES:] = (column == far).astype(F32).astype(BF16)
     predict_and_send(
-        0, star_ref, stiff_ref, proj_ref, send_ref, period_ref,
+        0, star_ref, stiff_ref, proj_ref, send_ref, None,
         derivs, table_ref, near_list_ref, far_list_ref, blocks, faces,
     )
 
@@ -243,11 +238,18 @@
 
 
 def own_first_kernel(
-    derivs, table_ref, star_ref, solver_ref, period_ref,
+    derivs, table_ref, star_ref, solver_ref, cluster_ref,
     stiffness_ref, projection_ref, lifting_ref, neighbor_ref, order_ref,
-    base_ref, partial_ref, both_ref, lift_ref, local_ref, remote_ref,
+    base_ref, partial_ref, both_ref, lift_ref, local_ref, remote_ref, period_ref,
     big, flux, work, work_lift,
 ):
+    lane = lax.broadcasted_iota(jnp.int32, (8, LANES), 1)
+    period = jnp.full((8, LANES), 1, jnp.int32)
+    for j in range(LANES // 16):
+        c = cluster_ref[j]
+        p = jnp.where(c == 0, 1, jnp.where(c == 1, 2, 4))
+        period = jnp.where((lane >> 4) == j, p, period)
+    period_ref[...] = period
     work[...] = jnp.zeros_like(work)
     for f in range(FACES):
         weights_into(work, f * FACE_ROWS, projection_ref[:, f, :], ROWS)
@@ -392,17 +394,16 @@
         pairs[(i // 2) % 2] .extend([(i, i + 2), (i + 2, i)])
     inner, outer = pairs
 
-    (derivs, table, near_list, far_list, stiff_w, proj_w, send_w, period) = call(
+    (derivs, table, near_list, far_list, stiff_w, proj_w, send_w) = call(
         begin_kernel, "begin",
-        (coefficients, star, stiffness, projection, block_cluster, send_faces),
+        (coefficients, star, stiffness, projection, send_faces),
         (
             DERIV, PAIRED, LIST, LIST,
             ((3 * ROWS, LANES), BF16), ((FACES * FACE_ROWS, LANES), BF16),
-            ((FACES * LANES, 2 * LANES), BF16), ((8, LANES), jnp.int32),
+            ((FACES * LANES, 2 * LANES), BF16),
         ),
         (BLOCKS, FACE, ((3 * ROWS, LANES), F32)),
         10**9,
-        [VMEM, VMEM, VMEM, VMEM, SMEM, VMEM],
     )
     sums = None
     for tick in range(TICKS):
@@ -413,18 +414,20 @@
         first_in = lax.ppermute(first, "region", outer)
         second_in = lax.ppermute(second, "region", inner)
         if tick == 0:
-            base, partial, both_w, lift_w, local_w, remote_w = call(
+            base, partial, both_w, lift_w, local_w, remote_w, period = call(
                 own_first_kernel, "own_first",
                 (
-                    derivs, table, star, solvers, period,
+                    derivs, table, star, solvers, block_cluster,
                     stiffness, projection, lifting, neighbors, first[:8],
                 ),
                 (
                     STATE, SUMS, ((BOTH_ROWS, LANES), BF16), ((ROWS, 192), BF16),
                     ((FACES * LANES, FACES * LANES), BF16), ((2 * LANES, FACES * LANES), BF16),
+                    ((8, LANES), jnp.int32),
                 ),
                 (BIG, FACE, ((BOTH_ROWS, LANES), F32), ((ROWS, 192), F32)),
                 10**9,
+                [VMEM] * 4 + [SMEM] + [VMEM] * 5,
             )
         else:
             base, partial = call(

time: 83.5 us -> 82.4 us (0.987)
  no operation moved by 1% of the time
where the time goes in v2:
time: 82.4 us; the launch traced here: 82 us
  starting transfers between devices  44.5 us (54%)
  Pallas kernels  18 us (22%)
  waiting for transfers between devices  9.55 us (12%)
  blocking collectives  7.78 us (9%)
  local copies, waits for them, and re-layouts  1.91 us (2%)
    ppermute x4, starting transfers between devices, per_device(): first_in = lax.ppermute(first, 'region', outer)  35.1 us
    pallas_call x13, Pallas kernels, call(): pl.pallas_call(kernel, name=name, out_shape=[jax.ShapeDtypeStruct(s, d) f...  18 us
    ppermute x4, waiting for transfers between devices, per_device(): second_in = lax.ppermute(second, 'region', inner)  9.54 us
    ppermute x4, starting transfers between devices, per_device(): second_in = lax.ppermute(second, 'region', inner)  9.42 us
    all_gather x4, blocking collectives, per_device(): gathered = lax.all_gather(near_list, 'region', axis_index_groups=cores)  7.78 us
    unnamed x19, local copies, waits for them, and re-layouts  1.9 us
  transfers between devices with their start and end apart: 8, of which 3 were waited for; matrix products, arithmetic and copies ran while one was open for 0% of the time, Pallas kernels for 6%

profile of v2, /device:TPU:6, one launch (start us, length us, event | category | flops | bytes accessed | tf_op | source)
XLA Modules:
  0.0 82.0 jit_solution(9466378570805691880)
XLA Ops:
  0.0 1.0 %copy.10.star_ref = f32[3,9,9,128]{3,2,1,0:T(8,128)S(1)} copy(f32[3,9,9,128]{3,0,2,1:T(4,128)} %param.10) | data formatting | bytes 248832 | tf_op args[1]
  1.0 0.0 copy-done
  1.1 2.5 %begin.1 = (f32[5,9,40,128]{3,2,1,0:T(8,128)S(1)}, bf16[288,512]{1,0:T(8,128)(2,1)S(1)}, f32[144,128]{1,0:T(8,128)S(1)}, f32[144,128]{1,0:T(8,128)S(1)}, bf16[12...) custom-call(f32[9,35,128]{2,1,0:T(8,128)S(1)} %copy-done, ...), custom_call_target="tpu_custom_call" | custom-call | flops 1000000000 | bytes 10000000 | tf_op jit(solution)/shard_map/begin/pallas_call | solution.py:363
  3.6 0.0 copy-start.6
  3.6 2.0 %all-gather = f32[288,128]{1,0:T(8,128)S(1)} all-gather(f32[144,128]{1,0:T(8,128)S(1)} %get-tuple-element.48), channel_id=2, replica_groups={{0,1},{2,3},{4,5},{6,7},{8,9},{10,11},{12,13},{14,15},{16,17},{18,19},{..., dimensions={0}, use_global_device_ids=true | all-gather | bytes 221184 | tf_op jit(solution)/shard_map/all_gather | solution.py:410
  5.7 3.5 %collective-permute-start.1 = (f32[144,128]{1,0:T(8,128)S(1)}, f32[144,128]{1,0:T(8,128)S(1)}, u32[]{:S(2)}, u32[]{:S(2)}) collective-permute-start(f32[144,128]{1,0:T(8,128)S(1)} %get-tuple-element.51), channel_id=1, source_target_pairs={{0,2},{2,0},{1,3},{3,1},{4,6},{6,4},{5,7},{7,5},{8,10},{10,8},{9,1... | collective-permute-start | bytes 221192 | tf_op jit(solution)/shard_map/ppermute | solution.py:415
  9.2 17.5 %collective-permute-start = (f32[144,128]{1,0:T(8,128)S(1)}, f32[144,128]{1,0:T(8,128)S(1)}, u32[]{:S(2)}, u32[]{:S(2)}) collective-permute-start(f32[144,128]{1,0:T(8,128)S(1)} %get-tuple-element.50), channel_id=1, source_target_pairs={{2,4},{4,2},{3,5},{5,3},{6,8},{8,6},{7,9},{9,7},{10,12},{12,10},{1... | collective-permute-start | bytes 221192 | tf_op jit(solution)/shard_map/ppermute | solution.py:414
  26.7 0.1 copy.13.lifting_ref
  26.9 0.1 copy.12.solver_ref
  26.9 0.0 copy-start.4
  26.9 0.0 copy-start.5
  26.9 0.7 copy-done.4
  27.6 2.0 %own_first.1 = (f32[9,40,128]{2,1,0:T(8,128)S(1)}, f32[144,512]{1,0:T(8,128)S(1)}, bf16[184,128]{1,0:T(8,128)(2,1)S(1)}, bf16[40,192]{1,0:T(8,128)(2,1)S(1)}, bf...) custom-call(f32[5,9,40,128]{3,2,1,0:T(8,128)S(1)} %get-tuple-element.52.derivs, ...), custom_call_target="tpu_custom_call" | custom-call | flops 1000000000 | bytes 10000000 | tf_op jit(solution)/shard_map/own_first/pallas_call | solution.py:363
  29.7 2.9 %step.3 = (f32[5,9,40,128]{3,2,1,0:T(8,128)S(1)}, f32[144,512]{1,0:T(8,128)S(1)}, bf16[288,512]{1,0:T(8,128)(2,1)S(1)}, f32[144,128]{1,0:T(8,128)S(1)}, f32[144,128]{1,0:T(8,128)S(1)}) custom-call(f32[144,128]{1,0:T(8,128)S(1)} %collective-permute-done.first_ref, f32[144,128]{1,0:T(8,128)S(1)} %collective-permute-done.1.second_ref, ...), custom_call_target="tpu_custom_call" | custom-call | flops 1000000000 | bytes 10000000 | tf_op jit(solution)/shard_map/step/pallas_call | solution.py:363
  32.6 1.9 %all-gather.1 = f32[288,128]{1,0:T(8,128)S(1)} all-gather(f32[144,128]{1,0:T(8,128)S(1)} %get-tuple-element.62), channel_id=3, replica_groups={{0,1},{2,3},{4,5},{6,7},{8,9},{10,11},{12,13},{14,15},{16,17},{18,19},{..., dimensions={0}, use_global_device_ids=true | all-gather | bytes 221184 | tf_op jit(solution)/shard_map/all_gather | solution.py:410
  34.6 7.5 %collective-permute-start.2 = (f32[144,128]{1,0:T(8,128)S(1)}, f32[144,128]{1,0:T(8,128)S(1)}, u32[]{:S(2)}, u32[]{:S(2)}) collective-permute-start(f32[144,128]{1,0:T(8,128)S(1)} %get-tuple-element.64), channel_id=1, source_target_pairs={{2,4},{4,2},{3,5},{5,3},{6,8},{8,6},{7,9},{9,7},{10,12},{12,10},{1... | collective-permute-start | bytes 221192 | tf_op jit(solution)/shard_map/ppermute | solution.py:414
  42.1 1.9 %collective-permute-start.3 = (f32[144,128]{1,0:T(8,128)S(1)}, f32[144,128]{1,0:T(8,128)S(1)}, u32[]{:S(2)}, u32[]{:S(2)}) collective-permute-start(f32[144,128]{1,0:T(8,128)S(1)} %get-tuple-element.65), channel_id=1, source_target_pairs={{0,2},{2,0},{1,3},{3,1},{4,6},{6,4},{5,7},{7,5},{8,10},{10,8},{9,1... | collective-permute-start | bytes 221192 | tf_op jit(solution)/shard_map/ppermute | solution.py:415
  44.0 1.1 %own.3 = (f32[9,40,128]{2,1,0:T(8,128)S(1)}, f32[144,512]{1,0:T(8,128)S(1)}) custom-call(f32[5,9,40,128]{3,2,1,0:T(8,128)S(1)} %get-tuple-element.66.derivs, bf16[288,512]{1,0:T(8,128)(2,1)S(1)} %get-tuple-element.67.table_ref, f32[144,512]{1,0:T(8,128)S(1)} %get-tuple-element.68.sum_ref, f32[3,9,9,128]{3,2,1,0:T(8,128)S(1)} %copy.10.star_ref, ...), custom_call_target="tpu_custom_call" | custom-call | flops 1000000000 | bytes 10000000 | tf_op jit(solution)/shard_map/own/pallas_call | solution.py:363
  45.1 3.2 %collective-permute-done.3.second_ref = f32[144,128]{1,0:T(8,128)S(1)} collective-permute-done((f32[144,128]{1,0:T(8,128)S(1)}, f32[144,128]{1,0:T(8,128)S(1)}, u32[]{:S(2)}, u32[]{:S(2)}) %collective-permute-start.3) | collective-permute-done | bytes 73760 | tf_op jit(solution)/shard_map/ppermute | solution.py:415
  48.3 2.9 %step.4 = (f32[5,9,40,128]{3,2,1,0:T(8,128)S(1)}, f32[144,512]{1,0:T(8,128)S(1)}, bf16[288,512]{1,0:T(8,128)(2,1)S(1)}, f32[144,128]{1,0:T(8,128)S(1)}, f32[144,128]{1,0:T(8,128)S(1)}) custom-call(f32[144,128]{1,0:T(8,128)S(1)} %collective-permute-done.2.first_ref, f32[144,128]{1,0:T(8,128)S(1)} %collective-permute-done.3.second_ref, ...), custom_call_target="tpu_custom_call" | custom-call | flops 1000000000 | bytes 10000000 | tf_op jit(solution)/shard_map/step/pallas_call | solution.py:363
  51.3 1.9 %all-gather.2 = f32[288,128]{1,0:T(8,128)S(1)} all-gather(f32[144,128]{1,0:T(8,128)S(1)} %get-tuple-element.73), channel_id=4, replica_groups={{0,1},{2,3},{4,5},{6,7},{8,9},{10,11},{12,13},{14,15},{16,17},{18,19},{..., dimensions={0}, use_global_device_ids=true | all-gather | bytes 221184 | tf_op jit(solution)/shard_map/all_gather | solution.py:410
  53.2 4.2 %collective-permute-start.4 = (f32[144,128]{1,0:T(8,128)S(1)}, f32[144,128]{1,0:T(8,128)S(1)}, u32[]{:S(2)}, u32[]{:S(2)}) collective-permute-start(f32[144,128]{1,0:T(8,128)S(1)} %get-tuple-element.75), channel_id=1, source_target_pairs={{2,4},{4,2},{3,5},{5,3},{6,8},{8,6},{7,9},{9,7},{10,12},{12,10},{1... | collective-permute-start | bytes 221192 | tf_op jit(solution)/shard_map/ppermute | solution.py:414
  57.4 2.1 %collective-permute-start.5 = (f32[144,128]{1,0:T(8,128)S(1)}, f32[144,128]{1,0:T(8,128)S(1)}, u32[]{:S(2)}, u32[]{:S(2)}) collective-permute-start(f32[144,128]{1,0:T(8,128)S(1)} %get-tuple-element.76), channel_id=1, source_target_pairs={{0,2},{2,0},{1,3},{3,1},{4,6},{6,4},{5,7},{7,5},{8,10},{10,8},{9,1... | collective-permute-start | bytes 221192 | tf_op jit(solution)/shard_map/ppermute | solution.py:415
  59.5 1.1 %own.4 = (f32[9,40,128]{2,1,0:T(8,128)S(1)}, f32[144,512]{1,0:T(8,128)S(1)}) custom-call(f32[5,9,40,128]{3,2,1,0:T(8,128)S(1)} %get-tuple-element.77.derivs, bf16[288,512]{1,0:T(8,128)(2,1)S(1)} %get-tuple-element.78.table_ref, f32[144,512]{1,0:T(8,128)S(1)} %get-tuple-element.79.sum_ref, f32[3,9,9,128]{3,2,1,0:T(8,128)S(1)} %copy.10.star_ref, ...), custom_call_target="tpu_custom_call" | custom-call | flops 1000000000 | bytes 10000000 | tf_op jit(solution)/shard_map/own/pallas_call | solution.py:363
  60.6 3.1 %collective-permute-done.5.second_ref = f32[144,128]{1,0:T(8,128)S(1)} collective-permute-done((f32[144,128]{1,0:T(8,128)S(1)}, f32[144,128]{1,0:T(8,128)S(1)}, u32[]{:S(2)}, u32[]{:S(2)}) %collective-permute-start.5) | collective-permute-done | bytes 73760 | tf_op jit(solution)/shard_map/ppermute | solution.py:415
  63.7 2.9 %step.5 = (f32[5,9,40,128]{3,2,1,0:T(8,128)S(1)}, f32[144,512]{1,0:T(8,128)S(1)}, bf16[288,512]{1,0:T(8,128)(2,1)S(1)}, f32[144,128]{1,0:T(8,128)S(1)}, f32[144,128]{1,0:T(8,128)S(1)}) custom-call(f32[144,128]{1,0:T(8,128)S(1)} %collective-permute-done.4.first_ref, f32[144,128]{1,0:T(8,128)S(1)} %collective-permute-done.5.second_ref, ...), custom_call_target="tpu_custom_call" | custom-call | flops 1000000000 | bytes 10000000 | tf_op jit(solution)/shard_map/step/pallas_call | solution.py:363
  66.6 1.9 %all-gather.3 = f32[288,128]{1,0:T(8,128)S(1)} all-gather(f32[144,128]{1,0:T(8,128)S(1)} %get-tuple-element.82), channel_id=5, replica_groups={{0,1},{2,3},{4,5},{6,7},{8,9},{10,11},{12,13},{14,15},{16,17},{18,19},{..., dimensions={0}, use_global_device_ids=true | all-gather | bytes 221184 | tf_op jit(solution)/shard_map/all_gather | solution.py:410
  68.6 5.9 %collective-permute-start.6 = (f32[144,128]{1,0:T(8,128)S(1)}, f32[144,128]{1,0:T(8,128)S(1)}, u32[]{:S(2)}, u32[]{:S(2)}) collective-permute-start(f32[144,128]{1,0:T(8,128)S(1)} %get-tuple-element.84), channel_id=1, source_target_pairs={{2,4},{4,2},{3,5},{5,3},{6,8},{8,6},{7,9},{9,7},{10,12},{12,10},{1... | collective-permute-start | bytes 221192 | tf_op jit(solution)/shard_map/ppermute | solution.py:414
  74.4 1.9 %collective-permute-start.7 = (f32[144,128]{1,0:T(8,128)S(1)}, f32[144,128]{1,0:T(8,128)S(1)}, u32[]{:S(2)}, u32[]{:S(2)}) collective-permute-start(f32[144,128]{1,0:T(8,128)S(1)} %get-tuple-element.85), channel_id=1, source_target_pairs={{0,2},{2,0},{1,3},{3,1},{4,6},{6,4},{5,7},{7,5},{8,10},{10,8},{9,1... | collective-permute-start | bytes 221192 | tf_op jit(solution)/shard_map/ppermute | solution.py:415
  76.4 1.1 %own.5 = (f32[9,40,128]{2,1,0:T(8,128)S(1)}, f32[144,512]{1,0:T(8,128)S(1)}) custom-call(f32[5,9,40,128]{3,2,1,0:T(8,128)S(1)} %get-tuple-element.86.derivs, bf16[288,512]{1,0:T(8,128)(2,1)S(1)} %get-tuple-element.87.table_ref, f32[144,512]{1,0:T(8,128)S(1)} %get-tuple-element.88.sum_ref, f32[3,9,9,128]{3,2,1,0:T(8,128)S(1)} %copy.10.star_ref, ...), custom_call_target="tpu_custom_call" | custom-call | flops 1000000000 | bytes 10000000 | tf_op jit(solution)/shard_map/own/pallas_call | solution.py:363
  77.5 3.2 %collective-permute-done.7.second_ref = f32[144,128]{1,0:T(8,128)S(1)} collective-permute-done((f32[144,128]{1,0:T(8,128)S(1)}, f32[144,128]{1,0:T(8,128)S(1)}, u32[]{:S(2)}, u32[]{:S(2)}) %collective-permute-start.7) | collective-permute-done | bytes 73760 | tf_op jit(solution)/shard_map/ppermute | solution.py:415
  80.7 1.3 %end.1 = f32[9,35,128]{2,1,0:T(8,128)} custom-call(f32[144,128]{1,0:T(8,128)S(1)} %collective-permute-done.6.first_ref, f32[144,128]{1,0:T(8,128)S(1)} %collective-permute-done.7.second_ref, f32[2,144,128]{2,1,0:T(8,128)S(1)} %bitcast.10, f32[9,40,128]{2,1,0:T(8,128)S(1)} %get-tuple-element.89.base_ref, f32[144,512]{1,0:T(8,128)S(1)} %get-tuple-element.90.partial_ref, ...), custom_call_target="tpu_custom_call" | custom-call | flops 1000000000 | bytes 10000000 | tf_op jit(solution)/shard_map/end/pallas_call | solution.py:363
  (24 shorter events, 0.1 us)
Async XLA Ops:
  0.0 1.0 %copy-start.1 = (f32[3,35,35]{2,1,0:T(8,128)S(1)}, f32[3,35,35]{2,1,0:T(8,128)}, u32[]{:S(2)}) copy-start(f32[3,35,35]{2,1,0:T(8,128)} %stiffness_ref.3) | copy-start | bytes 44104
  0.0 1.0 %copy-start.3 = (s32[4,64]{1,0:T(4,128)S(1)}, s32[4,64]{1,0:T(4,128)}, u32[]{:S(2)}) copy-start(s32[4,64]{1,0:T(4,128)} %faces_ref.1) | copy-start | bytes 3076
  0.0 1.0 %copy-start.2 = (f32[4,15,35]{2,0,1:T(4,128)S(1)}, f32[4,15,35]{2,0,1:T(4,128)}, u32[]{:S(2)}) copy-start(f32[4,15,35]{2,0,1:T(4,128)} %param.13) | copy-start | bytes 25204
  0.0 1.1 %copy-start = (f32[9,35,128]{2,1,0:T(8,128)S(1)}, f32[9,35,128]{2,1,0:T(8,128)}, u32[]{:S(2)}) copy-start(f32[9,35,128]{2,1,0:T(8,128)} %coef_ref.1) | copy-start | bytes 483844
  3.6 23.3 %copy-start.6 = (f32[2,4,9,9,128]{4,1,3,2,0:T(4,128)S(1)}, f32[2,4,9,9,128]{4,1,3,2,0:T(4,128)}, u32[]{:S(2)}) copy-start(f32[2,4,9,9,128]{4,1,3,2,0:T(4,128)} %param.11) | copy-start | bytes 995332
  5.7 21.1 %copy-start.7 = (f32[4,35,15]{1,0,2:T(4,128)S(1)}, f32[4,35,15]{1,0,2:T(4,128)}, u32[]{:S(2)}) copy-start(f32[4,35,15]{1,0,2:T(4,128)} %param.14) | copy-start | bytes 25204
  5.7 24.0 %collective-permute-start.1 = (f32[144,128]{1,0:T(8,128)S(1)}, f32[144,128]{1,0:T(8,128)S(1)}, u32[]{:S(2)}, u32[]{:S(2)}) collective-permute-start(f32[144,128]{1,0:T(8,128)S(1)} %get-tuple-element.51), channel_id=1, source_target_pairs={{0,2},{2,0},{1,3},{3,1},{4,6},{6,4},{5,7},{7,5},{8,10},{10,8},{9,1... | collective-permute-start | bytes 221192 | tf_op jit(solution)/shard_map/ppermute | solution.py:415
  9.2 20.5 %collective-permute-start = (f32[144,128]{1,0:T(8,128)S(1)}, f32[144,128]{1,0:T(8,128)S(1)}, u32[]{:S(2)}, u32[]{:S(2)}) collective-permute-start(f32[144,128]{1,0:T(8,128)S(1)} %get-tuple-element.50), channel_id=1, source_target_pairs={{2,4},{4,2},{3,5},{5,3},{6,8},{8,6},{7,9},{9,7},{10,12},{12,10},{1... | collective-permute-start | bytes 221192 | tf_op jit(solution)/shard_map/ppermute | solution.py:414
  26.9 0.7 copy-start.4
  26.9 0.7 copy-start.5
  34.6 13.7 %collective-permute-start.2 = (f32[144,128]{1,0:T(8,128)S(1)}, f32[144,128]{1,0:T(8,128)S(1)}, u32[]{:S(2)}, u32[]{:S(2)}) collective-permute-start(f32[144,128]{1,0:T(8,128)S(1)} %get-tuple-element.64), channel_id=1, source_target_pairs={{2,4},{4,2},{3,5},{5,3},{6,8},{8,6},{7,9},{9,7},{10,12},{12,10},{1... | collective-permute-start | bytes 221192 | tf_op jit(solution)/shard_map/ppermute | solution.py:414
  42.1 6.2 %collective-permute-start.3 = (f32[144,128]{1,0:T(8,128)S(1)}, f32[144,128]{1,0:T(8,128)S(1)}, u32[]{:S(2)}, u32[]{:S(2)}) collective-permute-start(f32[144,128]{1,0:T(8,128)S(1)} %get-tuple-element.65), channel_id=1, source_target_pairs={{0,2},{2,0},{1,3},{3,1},{4,6},{6,4},{5,7},{7,5},{8,10},{10,8},{9,1... | collective-permute-start | bytes 221192 | tf_op jit(solution)/shard_map/ppermute | solution.py:415
  53.2 10.5 %collective-permute-start.4 = (f32[144,128]{1,0:T(8,128)S(1)}, f32[144,128]{1,0:T(8,128)S(1)}, u32[]{:S(2)}, u32[]{:S(2)}) collective-permute-start(f32[144,128]{1,0:T(8,128)S(1)} %get-tuple-element.75), channel_id=1, source_target_pairs={{2,4},{4,2},{3,5},{5,3},{6,8},{8,6},{7,9},{9,7},{10,12},{12,10},{1... | collective-permute-start | bytes 221192 | tf_op jit(solution)/shard_map/ppermute | solution.py:414
  57.4 6.2 %collective-permute-start.5 = (f32[144,128]{1,0:T(8,128)S(1)}, f32[144,128]{1,0:T(8,128)S(1)}, u32[]{:S(2)}, u32[]{:S(2)}) collective-permute-start(f32[144,128]{1,0:T(8,128)S(1)} %get-tuple-element.76), channel_id=1, source_target_pairs={{0,2},{2,0},{1,3},{3,1},{4,6},{6,4},{5,7},{7,5},{8,10},{10,8},{9,1... | collective-permute-start | bytes 221192 | tf_op jit(solution)/shard_map/ppermute | solution.py:415
  68.6 12.1 %collective-permute-start.6 = (f32[144,128]{1,0:T(8,128)S(1)}, f32[144,128]{1,0:T(8,128)S(1)}, u32[]{:S(2)}, u32[]{:S(2)}) collective-permute-start(f32[144,128]{1,0:T(8,128)S(1)} %get-tuple-element.84), channel_id=1, source_target_pairs={{2,4},{4,2},{3,5},{5,3},{6,8},{8,6},{7,9},{9,7},{10,12},{12,10},{1... | collective-permute-start | bytes 221192 | tf_op jit(solution)/shard_map/ppermute | solution.py:414
  74.4 6.2 %collective-permute-start.7 = (f32[144,128]{1,0:T(8,128)S(1)}, f32[144,128]{1,0:T(8,128)S(1)}, u32[]{:S(2)}, u32[]{:S(2)}) collective-permute-start(f32[144,128]{1,0:T(8,128)S(1)} %get-tuple-element.85), channel_id=1, source_target_pairs={{0,2},{2,0},{1,3},{3,1},{4,6},{6,4},{5,7},{7,5},{8,10},{10,8},{9,1... | collective-permute-start | bytes 221192 | tf_op jit(solution)/shard_map/ppermute | solution.py:415

commit v3 on v2

--- a/solution.py
+++ b/solution.py
@@ -349,10 +349,8 @@
         tick, first_ref, second_ref, gathered_ref, base_ref, partial_ref, solver_ref, period_ref,
         lift_ref, remote_ref, sums, flux,
     )
-    ending = ending_mask(period_ref[0:1, :], tick)
     for p in range(NQ):
-        change = jnp.where(ending, lifted[:, p * LANES : (p + 1) * LANES], 0.0)
-        out_ref[p] = (base_ref[p] - change)[0:BASIS, :]
+        out_ref[p] = (base_ref[p] - lifted[:, p * LANES : (p + 1) * LANES])[0:BASIS, :]
 
 
 VMEM = pl.BlockSpec(memory_space=pltpu.VMEM)

time: 82.4 us -> 82.4 us (level)
  no operation moved by 1% of the time
where the time goes in v3:
time: 82.4 us; the launch traced here: 81.9 us
  starting transfers between devices  44.5 us (54%)
  Pallas kernels  17.9 us (22%)
  waiting for transfers between devices  9.55 us (12%)
  blocking collectives  7.78 us (9%)
  local copies, waits for them, and re-layouts  1.91 us (2%)
    ppermute x4, starting transfers between devices, per_device(): first_in = lax.ppermute(first, 'region', outer)  35.1 us
    pallas_call x13, Pallas kernels, call(): pl.pallas_call(kernel, name=name, out_shape=[jax.ShapeDtypeStruct(s, d) f...  17.9 us
    ppermute x4, waiting for transfers between devices, per_device(): second_in = lax.ppermute(second, 'region', inner)  9.54 us
    ppermute x4, starting transfers between devices, per_device(): second_in = lax.ppermute(second, 'region', inner)  9.42 us
    all_gather x4, blocking collectives, per_device(): gathered = lax.all_gather(near_list, 'region', axis_index_groups=cores)  7.78 us
    unnamed x19, local copies, waits for them, and re-layouts  1.9 us
  transfers between devices with their start and end apart: 8, of which 3 were waited for; matrix products, arithmetic and copies ran while one was open for 0% of the time, Pallas kernels for 6%

profile of v3, /device:TPU:6, one launch (start us, length us, event | category | flops | bytes accessed | tf_op | source)
XLA Modules:
  0.0 81.9 jit_solution(10804601914223960250)
XLA Ops:
  0.0 1.0 %copy.10.star_ref = f32[3,9,9,128]{3,2,1,0:T(8,128)S(1)} copy(f32[3,9,9,128]{3,0,2,1:T(4,128)} %param.10) | data formatting | bytes 248832 | tf_op args[1]
  1.0 0.0 copy-done
  1.1 2.5 %begin.1 = (f32[5,9,40,128]{3,2,1,0:T(8,128)S(1)}, bf16[288,512]{1,0:T(8,128)(2,1)S(1)}, f32[144,128]{1,0:T(8,128)S(1)}, f32[144,128]{1,0:T(8,128)S(1)}, bf16[12...) custom-call(f32[9,35,128]{2,1,0:T(8,128)S(1)} %copy-done, ...), custom_call_target="tpu_custom_call" | custom-call | flops 1000000000 | bytes 10000000 | tf_op jit(solution)/shard_map/begin/pallas_call | solution.py:361
  3.6 0.0 copy-start.6
  3.6 2.0 %all-gather = f32[288,128]{1,0:T(8,128)S(1)} all-gather(f32[144,128]{1,0:T(8,128)S(1)} %get-tuple-element.48), channel_id=2, replica_groups={{0,1},{2,3},{4,5},{6,7},{8,9},{10,11},{12,13},{14,15},{16,17},{18,19},{..., dimensions={0}, use_global_device_ids=true | all-gather | bytes 221184 | tf_op jit(solution)/shard_map/all_gather | solution.py:408
  5.7 3.5 %collective-permute-start.1 = (f32[144,128]{1,0:T(8,128)S(1)}, f32[144,128]{1,0:T(8,128)S(1)}, u32[]{:S(2)}, u32[]{:S(2)}) collective-permute-start(f32[144,128]{1,0:T(8,128)S(1)} %get-tuple-element.51), channel_id=1, source_target_pairs={{0,2},{2,0},{1,3},{3,1},{4,6},{6,4},{5,7},{7,5},{8,10},{10,8},{9,1... | collective-permute-start | bytes 221192 | tf_op jit(solution)/shard_map/ppermute | solution.py:413
  9.2 17.5 %collective-permute-start = (f32[144,128]{1,0:T(8,128)S(1)}, f32[144,128]{1,0:T(8,128)S(1)}, u32[]{:S(2)}, u32[]{:S(2)}) collective-permute-start(f32[144,128]{1,0:T(8,128)S(1)} %get-tuple-element.50), channel_id=1, source_target_pairs={{2,4},{4,2},{3,5},{5,3},{6,8},{8,6},{7,9},{9,7},{10,12},{12,10},{1... | collective-permute-start | bytes 221192 | tf_op jit(solution)/shard_map/ppermute | solution.py:412
  26.7 0.1 copy.13.lifting_ref
  26.9 0.1 copy.12.solver_ref
  26.9 0.0 copy-start.4
  26.9 0.0 copy-start.5
  26.9 0.7 copy-done.4
  27.6 2.0 %own_first.1 = (f32[9,40,128]{2,1,0:T(8,128)S(1)}, f32[144,512]{1,0:T(8,128)S(1)}, bf16[184,128]{1,0:T(8,128)(2,1)S(1)}, bf16[40,192]{1,0:T(8,128)(2,1)S(1)}, bf...) custom-call(f32[5,9,40,128]{3,2,1,0:T(8,128)S(1)} %get-tuple-element.52.derivs, ...), custom_call_target="tpu_custom_call" | custom-call | flops 1000000000 | bytes 10000000 | tf_op jit(solution)/shard_map/own_first/pallas_call | solution.py:361
  29.7 2.9 %step.3 = (f32[5,9,40,128]{3,2,1,0:T(8,128)S(1)}, f32[144,512]{1,0:T(8,128)S(1)}, bf16[288,512]{1,0:T(8,128)(2,1)S(1)}, f32[144,128]{1,0:T(8,128)S(1)}, f32[144,128]{1,0:T(8,128)S(1)}) custom-call(f32[144,128]{1,0:T(8,128)S(1)} %collective-permute-done.first_ref, f32[144,128]{1,0:T(8,128)S(1)} %collective-permute-done.1.second_ref, ...), custom_call_target="tpu_custom_call" | custom-call | flops 1000000000 | bytes 10000000 | tf_op jit(solution)/shard_map/step/pallas_call | solution.py:361
  32.6 1.9 %all-gather.1 = f32[288,128]{1,0:T(8,128)S(1)} all-gather(f32[144,128]{1,0:T(8,128)S(1)} %get-tuple-element.62), channel_id=3, replica_groups={{0,1},{2,3},{4,5},{6,7},{8,9},{10,11},{12,13},{14,15},{16,17},{18,19},{..., dimensions={0}, use_global_device_ids=true | all-gather | bytes 221184 | tf_op jit(solution)/shard_map/all_gather | solution.py:408
  34.6 7.5 %collective-permute-start.2 = (f32[144,128]{1,0:T(8,128)S(1)}, f32[144,128]{1,0:T(8,128)S(1)}, u32[]{:S(2)}, u32[]{:S(2)}) collective-permute-start(f32[144,128]{1,0:T(8,128)S(1)} %get-tuple-element.64), channel_id=1, source_target_pairs={{2,4},{4,2},{3,5},{5,3},{6,8},{8,6},{7,9},{9,7},{10,12},{12,10},{1... | collective-permute-start | bytes 221192 | tf_op jit(solution)/shard_map/ppermute | solution.py:412
  42.1 1.9 %collective-permute-start.3 = (f32[144,128]{1,0:T(8,128)S(1)}, f32[144,128]{1,0:T(8,128)S(1)}, u32[]{:S(2)}, u32[]{:S(2)}) collective-permute-start(f32[144,128]{1,0:T(8,128)S(1)} %get-tuple-element.65), channel_id=1, source_target_pairs={{0,2},{2,0},{1,3},{3,1},{4,6},{6,4},{5,7},{7,5},{8,10},{10,8},{9,1... | collective-permute-start | bytes 221192 | tf_op jit(solution)/shard_map/ppermute | solution.py:413
  44.0 1.1 %own.3 = (f32[9,40,128]{2,1,0:T(8,128)S(1)}, f32[144,512]{1,0:T(8,128)S(1)}) custom-call(f32[5,9,40,128]{3,2,1,0:T(8,128)S(1)} %get-tuple-element.66.derivs, bf16[288,512]{1,0:T(8,128)(2,1)S(1)} %get-tuple-element.67.table_ref, f32[144,512]{1,0:T(8,128)S(1)} %get-tuple-element.68.sum_ref, f32[3,9,9,128]{3,2,1,0:T(8,128)S(1)} %copy.10.star_ref, ...), custom_call_target="tpu_custom_call" | custom-call | flops 1000000000 | bytes 10000000 | tf_op jit(solution)/shard_map/own/pallas_call | solution.py:361
  45.1 3.2 %collective-permute-done.3.second_ref = f32[144,128]{1,0:T(8,128)S(1)} collective-permute-done((f32[144,128]{1,0:T(8,128)S(1)}, f32[144,128]{1,0:T(8,128)S(1)}, u32[]{:S(2)}, u32[]{:S(2)}) %collective-permute-start.3) | collective-permute-done | bytes 73760 | tf_op jit(solution)/shard_map/ppermute | solution.py:413
  48.3 2.9 %step.4 = (f32[5,9,40,128]{3,2,1,0:T(8,128)S(1)}, f32[144,512]{1,0:T(8,128)S(1)}, bf16[288,512]{1,0:T(8,128)(2,1)S(1)}, f32[144,128]{1,0:T(8,128)S(1)}, f32[144,128]{1,0:T(8,128)S(1)}) custom-call(f32[144,128]{1,0:T(8,128)S(1)} %collective-permute-done.2.first_ref, f32[144,128]{1,0:T(8,128)S(1)} %collective-permute-done.3.second_ref, ...), custom_call_target="tpu_custom_call" | custom-call | flops 1000000000 | bytes 10000000 | tf_op jit(solution)/shard_map/step/pallas_call | solution.py:361
  51.3 1.9 %all-gather.2 = f32[288,128]{1,0:T(8,128)S(1)} all-gather(f32[144,128]{1,0:T(8,128)S(1)} %get-tuple-element.73), channel_id=4, replica_groups={{0,1},{2,3},{4,5},{6,7},{8,9},{10,11},{12,13},{14,15},{16,17},{18,19},{..., dimensions={0}, use_global_device_ids=true | all-gather | bytes 221184 | tf_op jit(solution)/shard_map/all_gather | solution.py:408
  53.2 4.2 %collective-permute-start.4 = (f32[144,128]{1,0:T(8,128)S(1)}, f32[144,128]{1,0:T(8,128)S(1)}, u32[]{:S(2)}, u32[]{:S(2)}) collective-permute-start(f32[144,128]{1,0:T(8,128)S(1)} %get-tuple-element.75), channel_id=1, source_target_pairs={{2,4},{4,2},{3,5},{5,3},{6,8},{8,6},{7,9},{9,7},{10,12},{12,10},{1... | collective-permute-start | bytes 221192 | tf_op jit(solution)/shard_map/ppermute | solution.py:412
  57.4 2.1 %collective-permute-start.5 = (f32[144,128]{1,0:T(8,128)S(1)}, f32[144,128]{1,0:T(8,128)S(1)}, u32[]{:S(2)}, u32[]{:S(2)}) collective-permute-start(f32[144,128]{1,0:T(8,128)S(1)} %get-tuple-element.76), channel_id=1, source_target_pairs={{0,2},{2,0},{1,3},{3,1},{4,6},{6,4},{5,7},{7,5},{8,10},{10,8},{9,1... | collective-permute-start | bytes 221192 | tf_op jit(solution)/shard_map/ppermute | solution.py:413
  59.5 1.1 %own.4 = (f32[9,40,128]{2,1,0:T(8,128)S(1)}, f32[144,512]{1,0:T(8,128)S(1)}) custom-call(f32[5,9,40,128]{3,2,1,0:T(8,128)S(1)} %get-tuple-element.77.derivs, bf16[288,512]{1,0:T(8,128)(2,1)S(1)} %get-tuple-element.78.table_ref, f32[144,512]{1,0:T(8,128)S(1)} %get-tuple-element.79.sum_ref, f32[3,9,9,128]{3,2,1,0:T(8,128)S(1)} %copy.10.star_ref, ...), custom_call_target="tpu_custom_call" | custom-call | flops 1000000000 | bytes 10000000 | tf_op jit(solution)/shard_map/own/pallas_call | solution.py:361
  60.6 3.1 %collective-permute-done.5.second_ref = f32[144,128]{1,0:T(8,128)S(1)} collective-permute-done((f32[144,128]{1,0:T(8,128)S(1)}, f32[144,128]{1,0:T(8,128)S(1)}, u32[]{:S(2)}, u32[]{:S(2)}) %collective-permute-start.5) | collective-permute-done | bytes 73760 | tf_op jit(solution)/shard_map/ppermute | solution.py:413
  63.7 2.9 %step.5 = (f32[5,9,40,128]{3,2,1,0:T(8,128)S(1)}, f32[144,512]{1,0:T(8,128)S(1)}, bf16[288,512]{1,0:T(8,128)(2,1)S(1)}, f32[144,128]{1,0:T(8,128)S(1)}, f32[144,128]{1,0:T(8,128)S(1)}) custom-call(f32[144,128]{1,0:T(8,128)S(1)} %collective-permute-done.4.first_ref, f32[144,128]{1,0:T(8,128)S(1)} %collective-permute-done.5.second_ref, ...), custom_call_target="tpu_custom_call" | custom-call | flops 1000000000 | bytes 10000000 | tf_op jit(solution)/shard_map/step/pallas_call | solution.py:361
  66.6 1.9 %all-gather.3 = f32[288,128]{1,0:T(8,128)S(1)} all-gather(f32[144,128]{1,0:T(8,128)S(1)} %get-tuple-element.82), channel_id=5, replica_groups={{0,1},{2,3},{4,5},{6,7},{8,9},{10,11},{12,13},{14,15},{16,17},{18,19},{..., dimensions={0}, use_global_device_ids=true | all-gather | bytes 221184 | tf_op jit(solution)/shard_map/all_gather | solution.py:408
  68.6 5.9 %collective-permute-start.6 = (f32[144,128]{1,0:T(8,128)S(1)}, f32[144,128]{1,0:T(8,128)S(1)}, u32[]{:S(2)}, u32[]{:S(2)}) collective-permute-start(f32[144,128]{1,0:T(8,128)S(1)} %get-tuple-element.84), channel_id=1, source_target_pairs={{2,4},{4,2},{3,5},{5,3},{6,8},{8,6},{7,9},{9,7},{10,12},{12,10},{1... | collective-permute-start | bytes 221192 | tf_op jit(solution)/shard_map/ppermute | solution.py:412
  74.4 1.9 %collective-permute-start.7 = (f32[144,128]{1,0:T(8,128)S(1)}, f32[144,128]{1,0:T(8,128)S(1)}, u32[]{:S(2)}, u32[]{:S(2)}) collective-permute-start(f32[144,128]{1,0:T(8,128)S(1)} %get-tuple-element.85), channel_id=1, source_target_pairs={{0,2},{2,0},{1,3},{3,1},{4,6},{6,4},{5,7},{7,5},{8,10},{10,8},{9,1... | collective-permute-start | bytes 221192 | tf_op jit(solution)/shard_map/ppermute | solution.py:413
  76.4 1.1 %own.5 = (f32[9,40,128]{2,1,0:T(8,128)S(1)}, f32[144,512]{1,0:T(8,128)S(1)}) custom-call(f32[5,9,40,128]{3,2,1,0:T(8,128)S(1)} %get-tuple-element.86.derivs, bf16[288,512]{1,0:T(8,128)(2,1)S(1)} %get-tuple-element.87.table_ref, f32[144,512]{1,0:T(8,128)S(1)} %get-tuple-element.88.sum_ref, f32[3,9,9,128]{3,2,1,0:T(8,128)S(1)} %copy.10.star_ref, ...), custom_call_target="tpu_custom_call" | custom-call | flops 1000000000 | bytes 10000000 | tf_op jit(solution)/shard_map/own/pallas_call | solution.py:361
  77.5 3.2 %collective-permute-done.7.second_ref = f32[144,128]{1,0:T(8,128)S(1)} collective-permute-done((f32[144,128]{1,0:T(8,128)S(1)}, f32[144,128]{1,0:T(8,128)S(1)}, u32[]{:S(2)}, u32[]{:S(2)}) %collective-permute-start.7) | collective-permute-done | bytes 73760 | tf_op jit(solution)/shard_map/ppermute | solution.py:413
  80.7 1.3 %end.1 = f32[9,35,128]{2,1,0:T(8,128)} custom-call(f32[144,128]{1,0:T(8,128)S(1)} %collective-permute-done.6.first_ref, f32[144,128]{1,0:T(8,128)S(1)} %collective-permute-done.7.second_ref, f32[2,144,128]{2,1,0:T(8,128)S(1)} %bitcast.10, f32[9,40,128]{2,1,0:T(8,128)S(1)} %get-tuple-element.89.base_ref, f32[144,512]{1,0:T(8,128)S(1)} %get-tuple-element.90.partial_ref, ...), custom_call_target="tpu_custom_call" | custom-call | flops 1000000000 | bytes 10000000 | tf_op jit(solution)/shard_map/end/pallas_call | solution.py:361
  (24 shorter events, 0.1 us)
Async XLA Ops:
  0.0 1.0 %copy-start.1 = (f32[3,35,35]{2,1,0:T(8,128)S(1)}, f32[3,35,35]{2,1,0:T(8,128)}, u32[]{:S(2)}) copy-start(f32[3,35,35]{2,1,0:T(8,128)} %stiffness_ref.3) | copy-start | bytes 44104
  0.0 1.0 %copy-start.3 = (s32[4,64]{1,0:T(4,128)S(1)}, s32[4,64]{1,0:T(4,128)}, u32[]{:S(2)}) copy-start(s32[4,64]{1,0:T(4,128)} %faces_ref.1) | copy-start | bytes 3076
  0.0 1.0 %copy-start.2 = (f32[4,15,35]{2,0,1:T(4,128)S(1)}, f32[4,15,35]{2,0,1:T(4,128)}, u32[]{:S(2)}) copy-start(f32[4,15,35]{2,0,1:T(4,128)} %param.13) | copy-start | bytes 25204
  0.0 1.1 %copy-start = (f32[9,35,128]{2,1,0:T(8,128)S(1)}, f32[9,35,128]{2,1,0:T(8,128)}, u32[]{:S(2)}) copy-start(f32[9,35,128]{2,1,0:T(8,128)} %coef_ref.1) | copy-start | bytes 483844
  3.6 23.3 %copy-start.6 = (f32[2,4,9,9,128]{4,1,3,2,0:T(4,128)S(1)}, f32[2,4,9,9,128]{4,1,3,2,0:T(4,128)}, u32[]{:S(2)}) copy-start(f32[2,4,9,9,128]{4,1,3,2,0:T(4,128)} %param.11) | copy-start | bytes 995332
  5.7 21.1 %copy-start.7 = (f32[4,35,15]{1,0,2:T(4,128)S(1)}, f32[4,35,15]{1,0,2:T(4,128)}, u32[]{:S(2)}) copy-start(f32[4,35,15]{1,0,2:T(4,128)} %param.14) | copy-start | bytes 25204
  5.7 24.0 %collective-permute-start.1 = (f32[144,128]{1,0:T(8,128)S(1)}, f32[144,128]{1,0:T(8,128)S(1)}, u32[]{:S(2)}, u32[]{:S(2)}) collective-permute-start(f32[144,128]{1,0:T(8,128)S(1)} %get-tuple-element.51), channel_id=1, source_target_pairs={{0,2},{2,0},{1,3},{3,1},{4,6},{6,4},{5,7},{7,5},{8,10},{10,8},{9,1... | collective-permute-start | bytes 221192 | tf_op jit(solution)/shard_map/ppermute | solution.py:413
  9.2 20.5 %collective-permute-start = (f32[144,128]{1,0:T(8,128)S(1)}, f32[144,128]{1,0:T(8,128)S(1)}, u32[]{:S(2)}, u32[]{:S(2)}) collective-permute-start(f32[144,128]{1,0:T(8,128)S(1)} %get-tuple-element.50), channel_id=1, source_target_pairs={{2,4},{4,2},{3,5},{5,3},{6,8},{8,6},{7,9},{9,7},{10,12},{12,10},{1... | collective-permute-start | bytes 221192 | tf_op jit(solution)/shard_map/ppermute | solution.py:412
  26.9 0.7 copy-start.4
  26.9 0.7 copy-start.5
  34.6 13.7 %collective-permute-start.2 = (f32[144,128]{1,0:T(8,128)S(1)}, f32[144,128]{1,0:T(8,128)S(1)}, u32[]{:S(2)}, u32[]{:S(2)}) collective-permute-start(f32[144,128]{1,0:T(8,128)S(1)} %get-tuple-element.64), channel_id=1, source_target_pairs={{2,4},{4,2},{3,5},{5,3},{6,8},{8,6},{7,9},{9,7},{10,12},{12,10},{1... | collective-permute-start | bytes 221192 | tf_op jit(solution)/shard_map/ppermute | solution.py:412
  42.1 6.2 %collective-permute-start.3 = (f32[144,128]{1,0:T(8,128)S(1)}, f32[144,128]{1,0:T(8,128)S(1)}, u32[]{:S(2)}, u32[]{:S(2)}) collective-permute-start(f32[144,128]{1,0:T(8,128)S(1)} %get-tuple-element.65), channel_id=1, source_target_pairs={{0,2},{2,0},{1,3},{3,1},{4,6},{6,4},{5,7},{7,5},{8,10},{10,8},{9,1... | collective-permute-start | bytes 221192 | tf_op jit(solution)/shard_map/ppermute | solution.py:413
  53.2 10.5 %collective-permute-start.4 = (f32[144,128]{1,0:T(8,128)S(1)}, f32[144,128]{1,0:T(8,128)S(1)}, u32[]{:S(2)}, u32[]{:S(2)}) collective-permute-start(f32[144,128]{1,0:T(8,128)S(1)} %get-tuple-element.75), channel_id=1, source_target_pairs={{2,4},{4,2},{3,5},{5,3},{6,8},{8,6},{7,9},{9,7},{10,12},{12,10},{1... | collective-permute-start | bytes 221192 | tf_op jit(solution)/shard_map/ppermute | solution.py:412
  57.4 6.2 %collective-permute-start.5 = (f32[144,128]{1,0:T(8,128)S(1)}, f32[144,128]{1,0:T(8,128)S(1)}, u32[]{:S(2)}, u32[]{:S(2)}) collective-permute-start(f32[144,128]{1,0:T(8,128)S(1)} %get-tuple-element.76), channel_id=1, source_target_pairs={{0,2},{2,0},{1,3},{3,1},{4,6},{6,4},{5,7},{7,5},{8,10},{10,8},{9,1... | collective-permute-start | bytes 221192 | tf_op jit(solution)/shard_map/ppermute | solution.py:413
  68.6 12.1 %collective-permute-start.6 = (f32[144,128]{1,0:T(8,128)S(1)}, f32[144,128]{1,0:T(8,128)S(1)}, u32[]{:S(2)}, u32[]{:S(2)}) collective-permute-start(f32[144,128]{1,0:T(8,128)S(1)} %get-tuple-element.84), channel_id=1, source_target_pairs={{2,4},{4,2},{3,5},{5,3},{6,8},{8,6},{7,9},{9,7},{10,12},{12,10},{1... | collective-permute-start | bytes 221192 | tf_op jit(solution)/shard_map/ppermute | solution.py:412
  74.4 6.2 %collective-permute-start.7 = (f32[144,128]{1,0:T(8,128)S(1)}, f32[144,128]{1,0:T(8,128)S(1)}, u32[]{:S(2)}, u32[]{:S(2)}) collective-permute-start(f32[144,128]{1,0:T(8,128)S(1)} %get-tuple-element.85), channel_id=1, source_target_pairs={{0,2},{2,0},{1,3},{3,1},{4,6},{6,4},{5,7},{7,5},{8,10},{10,8},{9,1... | collective-permute-start | bytes 221192 | tf_op jit(solution)/shard_map/ppermute | solution.py:413
